TPU v7x, 128 devices: a whole 4x4x4 slice. The times are simulated.
128 devices in a mesh: gx: 8 (over y, core), gy: 16 (over x, z).
Axes of the slice: x: 4, y: 4, z: 4, core: 2. Of those that a mesh axis runs over, the one named last changes fastest.
Arguments:
- child_value: bfloat16 [2097152, 128], P(('gx', 'gy')), may hold values from -6 to 6
- child_row: int32 [128, 16384], P(('gx', 'gy')), may hold values from 0 to 16383, each once within a row
- opp_set: int32 [2097152], P(('gx', 'gy')), may hold values from 0 to 262143, as said below
- opp_home: int32 [262144], replicated, may hold values from 0 to 262143, as said below
- opp_cum: float32 [262144, 128], P(('gx', 'gy')), may hold values from 0.01 to 1
- reach: float32 [16384], P(('gx', 'gy')), may hold values from 0.05 to 1
- br_set: int32 [16384], P(('gx', 'gy')), may hold values from 0 to 8191, as said below
- br_home: int32 [8192], replicated, may hold values from 0 to 8191, as said below
- br_cum: float32 [8192, 128], P(('gx', 'gy')), may hold values from 0.01 to 1
Outputs:
- history_value: float32 [2097152], P(('gx', 'gy'))
- regret_gap: float32 [8192], P(('gx', 'gy'))
- exploitability: float32 [], replicated
Inputs may be any that keep to these rules, and one draw needn't show every extreme that they name: A permutation: opponent infoset i lives in row opp_home[i], owned by device opp_home[i] // 2048. `opp_set`: among the 16384 rows of one device at most 256 have infosets owned by any one device; in every draw some owner has exactly 256 from every device. A permutation: best-responder infoset i lives in row br_home[i], owned by device br_home[i] // 64. `br_set`: among the 128 rows of one device at most 2 have infosets owned by any one device; in every draw some owner has exactly 2 from every device.
All inputs are finite; a program needn't handle non-finite values.
Results may differ from a plain program's by a relative error of at most 0.0029.
Values may be sent and summed in bfloat16 or wider, within the bound.
A program may use at most 128 MiB of HBM per device.

v0:
```python
import functools

import jax
import jax.numpy as jnp
from jax import lax
from jax.sharding import Mesh
from jax.sharding import PartitionSpec as P

GX_GY = ("gx_0", "gx_1", "gy_0", "gy_1")
GX = ("gx_0", "gx_1")
GY = ("gy_0", "gy_1")


def in_one_piece(arrays, axis, split_dim, concat_dim, along):
    ends, at = ([], 0)
    for a in arrays[:-1]:
        at += a.shape[along]
        ends.append(at)
    both = jnp.concatenate(arrays, axis=along)
    return tuple(
        jnp.split(
            lax.all_to_all(both, axis, split_axis=split_dim, concat_axis=concat_dim, tiled=True),
            ends,
            axis=along,
        )
    )


def one_axis_at_a_time(value, axes):
    return functools.reduce(lax.psum, axes, value)


def arrival_rank(owner, count):
    rows = owner.shape[0]
    block = min(rows, 128)
    marks = (owner[:, None] == jnp.arange(count, dtype=jnp.int32)[None, :]).astype(jnp.float32)
    marks = marks.reshape(rows // block, block, count)
    lower = (jnp.arange(block)[:, None] > jnp.arange(block)[None, :]).astype(jnp.float32)
    within = jnp.einsum("ij,bjd->bid", lower, marks, precision=lax.Precision.HIGHEST)
    per_block = jnp.sum(marks, axis=1)
    before = jnp.cumsum(per_block, axis=0) - per_block
    rank = jnp.sum((within + before[:, None, :]) * marks, axis=2).reshape(rows)
    return rank.astype(jnp.int32)


def slot_source(place, slots):
    rows = place.shape[0]
    source = jnp.full((slots,), rows, jnp.int32).at[place].set(jnp.arange(rows, dtype=jnp.int32))
    filled = source < rows
    return (jnp.minimum(source, rows - 1), filled)


def fill_slots(table, source, filled):
    rows = jnp.take(table, source, axis=0)
    return jnp.where(filled[:, None], rows, jnp.zeros_like(rows))


def move_rows(blocks):
    return lax.all_to_all(blocks, GX_GY, split_axis=0, concat_axis=0, tiled=True)


def local(child_value, child_row, opp_set, opp_home, opp_cum, reach, br_set, br_home, br_cum):
    across = lax.axis_size(GX)
    along = lax.axis_size(GY)
    devices = across * along
    hist, acts = child_value.shape
    parents = reach.shape[0]
    per_opp = opp_cum.shape[0]
    per_br = br_cum.shape[0]
    limit = max(2, (2 * hist + devices - 1) // devices)
    limit_two = max(2, (2 * parents + devices - 1) // devices)
    home = jnp.take(opp_home, opp_set)
    owner = home // per_opp
    place = owner * limit + arrival_rank(owner, devices)
    home_two = jnp.take(br_home, br_set)
    owner_two = home_two // per_br
    place_two = owner_two * limit_two + arrival_rank(owner_two, devices)
    source, filled = slot_source(place, devices * limit)
    source_two, filled_two = slot_source(place_two, devices * limit_two)
    wanted = jnp.where(filled, jnp.take(home % per_opp, source), -1)
    wanted_two = jnp.where(filled_two, jnp.take(home_two % per_br, source_two), -1)
    asked, asked_two = in_one_piece(
        (wanted.reshape(devices, limit), wanted_two.reshape(devices, limit_two)), GX_GY, 0, 0, 1
    )
    asked = jnp.maximum(asked.reshape(-1), 0)
    asked_two = asked_two.reshape(-1)
    policy = (opp_cum / jnp.sum(opp_cum, axis=1, keepdims=True)).astype(jnp.bfloat16)
    served = jnp.take(policy, asked, axis=0).reshape(devices, limit, acts)
    fetched = move_rows(served).reshape(devices * limit, acts)
    mine = jnp.take(fetched, place, axis=0)
    history_value = jnp.einsum("ra,ra->r", mine, child_value, preferred_element_type=jnp.float32)
    chosen = jnp.take(history_value, child_row.reshape(-1)).reshape(parents, acts)
    weighted = reach[:, None] * chosen
    outgoing_two = fill_slots(weighted, source_two, filled_two)
    incoming_two = lax.all_to_all(
        outgoing_two.reshape(devices, limit_two, acts),
        GX_GY,
        split_axis=0,
        concat_axis=0,
        tiled=True,
    )
    incoming_two = incoming_two.reshape(devices * limit_two, acts)
    member = (asked_two[None, :] == jnp.arange(per_br, dtype=jnp.int32)[:, None]).astype(
        jnp.float32
    )
    action_value = jnp.dot(member, incoming_two, precision=lax.Precision.HIGHEST)
    br_policy = br_cum / jnp.sum(br_cum, axis=1, keepdims=True)
    regret_gap = jnp.max(action_value, axis=1) - jnp.sum(br_policy * action_value, axis=1)
    gap_total, reach_total = (
        one_axis_at_a_time(jnp.sum(regret_gap), GX_GY),
        one_axis_at_a_time(jnp.sum(reach), GX_GY),
    )
    return (history_value, regret_gap, gap_total / reach_total)


def solution(mesh):
    torus = Mesh(mesh.devices.reshape(4, 2, 4, 4), ("gx_0", "gx_1", "gy_0", "gy_1"))
    placed = (
        P(GX_GY, None),
        P(GX_GY, None),
        P(GX_GY),
        P(),
        P(GX_GY, None),
        P(GX_GY),
        P(GX_GY),
        P(),
        P(GX_GY, None),
    )
    return jax.shard_map(
        local, mesh=torus, in_specs=placed, out_specs=(P(GX_GY), P(GX_GY), P()), check_vma=False
    )
```

profile of v0, /device:TPU:0, one launch (start us, length us, event | category | flops | bytes accessed | tf_op | source)
XLA Modules:
  0.0 809.5 jit_solution(8699927011402245312)
XLA Ops:
  0.6 0.0 copy-start
  0.6 0.7 compare_select_fusion.7
  1.4 1.7 gather_fusion.2
  3.1 0.7 and_select_fusion.1
  3.8 0.7 and_select_fusion.2
  4.4 0.1 convert_reduce_fusion.1
  4.5 0.3 fusion.7
  4.8 1.0 scatter_custom_fusion.1
  5.9 1.9 gather_fusion.3
  7.7 0.1 reshape.286
  7.9 0.9 fusion.17
  8.7 0.0 copy-done
  8.8 0.0 copy-start.3
  8.8 90.5 %gather_fusion = s32[16384]{0:T(1024)S(1)} fusion(s32[262144]{0:T(1024)S(1)} %copy-done, s32[16384]{0:T(1024)S(1)} %fusion.17), kind=kCustom, calls=%fused_computation | custom fusion | bytes 196608 | tf_op jit(solution)/shard_map/jit(_take)/gather | solution.py:72
  99.3 0.0 copy-done.3
  99.3 0.1 fusion.24
  99.4 1.4 convert_reduce_fusion
  100.8 0.2 reduce_window_sum.17
  100.9 3.2 fusion.1
  104.2 0.1 compare_and_fusion
  104.3 60.4 %scatter_custom_fusion = s32[32768]{0:T(1024)S(1)} fusion(s32[16384]{0:T(1024)S(1)} %get-tuple-element.16, s32[16384]{0:T(1024)S(1)} %iota.39, s32[]{:T(128)} %constant.177.clone.1), kind=kCustom, calls=%fused_computation.49 | custom fusion | bytes 131076 | tf_op jit(solution)/shard_map/scatter | solution.py:48
  164.7 0.0 copy-start.2
  164.7 180.5 %gather_fusion.1 = s32[32768]{0:T(1024)S(1)} fusion(s32[16384]{0:T(1024)S(1)} %get-tuple-element.23, s32[32768]{0:T(1024)S(1)} %fusion.8), kind=kCustom, calls=%fused_computation.1 | custom fusion | bytes 393216 | tf_op jit(solution)/shard_map/jit(_take)/gather | solution.py:80
  345.3 0.1 select_select_fusion.1
  345.4 0.9 copy.18
  346.3 11.2 %all-to-all-start = ((s32[128,1,258]{2,1,0:T(1,128)}), s32[128,1,258]{2,1,0:T(1,128)S(1)}, u32[]{:S(2)}, u32[]{:S(2)}) async-start(s32[128,1,258]{2,1,0:T(1,128)} %copy.18), calls=%async_computation | async-start | bytes 393216 | tf_op jit(solution)/shard_map/all_to_all | solution.py:22
  357.4 0.0 copy-done.2
  357.5 0.3 reduce_sum.85
  357.8 0.3 divide_convert_fusion
  358.2 9.5 %all-to-all-done = s32[128,1,258]{2,1,0:T(1,128)S(1)} async-done(((s32[128,1,258]{2,1,0:T(1,128)}), s32[128,1,258]{2,1,0:T(1,128)S(1)}, u32[]{:S(2)}, u32[]{:S(2)}) %all-to-all-start) | async-done | bytes 132128 | tf_op jit(solution)/shard_map/all_to_all | solution.py:22
  367.6 0.1 copy.19
  367.8 0.1 copy.21
  367.9 0.1 copy.30
  368.0 0.1 copy.20
  368.1 114.2 %gather_fusion.4 = bf16[32768,128]{1,0:T(8,128)(2,1)} fusion(bf16[2048,128]{1,0:T(8,128)(2,1)S(1)} %divide_convert_fusion, s32[32768]{0:T(1024)S(1)} %broadcast_clamp_fusion), kind=kCustom, calls=%fused_computation.4 | custom fusion | bytes 16908288 | tf_op jit(solution)/shard_map/jit(_take)/gather | solution.py:88
  482.3 7.6 broadcast_select_fusion
  489.9 6.3 all-to-all-start.1
  496.2 0.2 broadcast_in_dim.124
  496.4 0.2 broadcast_in_dim.122
  496.5 0.0 copy-done.4
  496.5 0.1 compare_select_fusion
  496.6 99.3 %all-to-all-done.1 = bf16[128,256,128]{2,1,0:T(8,128)(2,1)} async-done(((bf16[128,256,128]{2,1,0:T(8,128)(2,1)}), bf16[128,256,128]{2,1,0:T(8,128)(2,1)}, u32[]{:S(2)}, u32[]{:S(2)}) %all-to-all-start.1) | async-done | bytes 8388640 | tf_op jit(solution)/shard_map/all_to_all | solution.py:59
  595.9 59.4 %gather_fusion.5 = bf16[16384,128]{1,0:T(8,128)(2,1)} fusion(bf16[32768,128]{1,0:T(8,128)(2,1)} %bitcast.9, s32[16384]{0:T(1024)S(1)} %broadcast_clamp_fusion.2), kind=kCustom, calls=%fused_computation.5 | custom fusion | bytes 8454144 | tf_op jit(solution)/shard_map/jit(_take)/gather | solution.py:90
  655.3 8.2 %fusion = f32[16384]{0:T(1024)S(1)} fusion(bf16[16384,128]{1,0:T(8,128)(2,1)} %param.9, bf16[16384,128]{1,0:T(8,128)(2,1)} %gather_fusion.5, pred[16384]{0:T(1024)(128)(4,1)S(1)} %get-tuple-element.15), kind=kLoop, calls=%fused_computation.11 | loop fusion | flops 10469376 | bytes 8470528 | tf_op jit(solution)/shard_map/ra,ra->r/dot_general | solution.py:91
  663.5 0.0 copy-start.1
  663.5 0.0 copy-start.6
  663.5 0.0 copy-start.5
  663.5 90.5 %gather_fusion.6 = f32[16384]{0:T(1024)S(1)} fusion(f32[16384]{0:T(1024)S(1)} %fusion, s32[16384]{0:T(1024)S(1)} %broadcast_clamp_fusion.1), kind=kCustom, calls=%fused_computation.6 | custom fusion | bytes 196608 | tf_op jit(solution)/shard_map/jit(_take)/gather | solution.py:92
  754.1 0.0 copy-done.1
  754.1 0.1 fusion.9
  754.2 0.7 gather_fusion.7
  754.9 1.0 select_select_fusion
  755.9 9.0 %all-to-all-start.2 = ((f32[128,2,128]{2,1,0:T(2,128)}), f32[128,2,128]{2,1,0:T(2,128)S(1)}, u32[]{:S(2)}, u32[]{:S(2)}) async-start(f32[128,2,128]{2,1,0:T(2,128)} %select_select_fusion), calls=%async_computation.2 | async-start | bytes 262144 | tf_op jit(solution)/shard_map/all_to_all | solution.py:95
  764.9 0.6 reduce_sum.89
  765.5 0.1 reduce_sum.86
  765.6 0.1 copy.22
  765.8 0.1 eq.71
  765.9 8.6 %all-to-all-done.2 = f32[128,2,128]{2,1,0:T(2,128)S(1)} async-done(((f32[128,2,128]{2,1,0:T(2,128)}), f32[128,2,128]{2,1,0:T(2,128)S(1)}, u32[]{:S(2)}, u32[]{:S(2)}) %all-to-all-start.2) | async-done | bytes 131104 | tf_op jit(solution)/shard_map/all_to_all | solution.py:95
  774.5 0.3 multiply_reduce_fusion
  774.8 1.1 fusion.25
  775.9 9.4 %all-reduce.2 = (f32[]{:T(128)}, f32[]{:T(128)}) all-reduce(f32[]{:T(128)} %get-tuple-element.13, f32[]{:T(128)} %reduce_sum.89), channel_id=1, replica_groups=mesh['gx_0'=4,'gx_1'=2,'gy_0'=4,'gy_1'=4] {'gx_0'}, use_global_device_ids=true, to_apply=%region_12.13 | all-reduce | flops 2 | bytes 16 | tf_op jit(solution)/shard_map/psum | solution.py:30
  785.4 3.2 all-reduce.3
  788.5 8.9 %all-reduce.1 = (f32[]{:T(128)}, f32[]{:T(128)}) all-reduce(f32[]{:T(128)} %get-tuple-element.11, f32[]{:T(128)} %get-tuple-element.12), channel_id=1, replica_groups=mesh['gx_0'=4,'gx_1'=2,'gy_0'=4,'gy_1'=4] {'gy_0'}, use_global_device_ids=true, to_apply=%region_14.15 | all-reduce | flops 2 | bytes 16 | tf_op jit(solution)/shard_map/psum | solution.py:30
  797.5 9.6 %all-reduce = (f32[]{:T(128)}, f32[]{:T(128)}) all-reduce(f32[]{:T(128)} %get-tuple-element.7, f32[]{:T(128)} %get-tuple-element.8), channel_id=1, replica_groups=mesh['gx_0'=4,'gx_1'=2,'gy_0'=4,'gy_1'=4] {'gy_1'}, use_global_device_ids=true, to_apply=%region_15.16 | all-reduce | flops 2 | bytes 16 | tf_op jit(solution)/shard_map/psum | solution.py:30
  (21 shorter events, 0.3 us)
Async XLA Ops:
  0.6 8.1 %copy-start = (s32[262144]{0:T(1024)S(1)}, s32[262144]{0:T(1024)}, u32[]{:S(2)}) copy-start(s32[262144]{0:T(1024)} %param.12) | copy-start | bytes 3145732
  8.8 90.6 %copy-start.3 = (s32[16384]{0:T(1024)S(1)}, s32[16384]{0:T(1024)}, u32[]{:S(2)}) copy-start(s32[16384]{0:T(1024)} %param.11) | copy-start | bytes 196612
  164.7 192.7 %copy-start.2 = (f32[2048,128]{1,0:T(8,128)S(1)}, f32[2048,128]{1,0:T(8,128)}, u32[]{:S(2)}) copy-start(f32[2048,128]{1,0:T(8,128)} %param.13) | copy-start | bytes 3145732
  346.3 21.4 %all-to-all-start = ((s32[128,1,258]{2,1,0:T(1,128)}), s32[128,1,258]{2,1,0:T(1,128)S(1)}, u32[]{:S(2)}, u32[]{:S(2)}) async-start(s32[128,1,258]{2,1,0:T(1,128)} %copy.18), calls=%async_computation | async-start | bytes 393216 | tf_op jit(solution)/shard_map/all_to_all | solution.py:22
  489.9 6.6 copy-start.4
  489.9 106.0 %all-to-all-start.1 = ((bf16[128,256,128]{2,1,0:T(8,128)(2,1)}), bf16[128,256,128]{2,1,0:T(8,128)(2,1)}, u32[]{:S(2)}, u32[]{:S(2)}) async-start(bf16[128,256,128]{2,1,0:T(8,128)(2,1)} %broadcast_select_fusion), calls=%async_computation.1 | async-start | bytes 16777216 | tf_op jit(solution)/shard_map/all_to_all | solution.py:59
  663.5 90.6 %copy-start.1 = (f32[16384]{0:T(1024)}, f32[16384]{0:T(1024)S(1)}, u32[]{:S(2)}) copy-start(f32[16384]{0:T(1024)S(1)} %fusion) | copy-start | bytes 196612
  663.5 90.6 %copy-start.6 = (f32[128]{0:T(128)S(1)}, f32[128]{0:T(128)}, u32[]{:S(2)}) copy-start(f32[128]{0:T(128)} %param.14) | copy-start | bytes 1540
  663.5 102.0 %copy-start.5 = (f32[64,128]{1,0:T(8,128)S(1)}, f32[64,128]{1,0:T(8,128)}, u32[]{:S(2)}) copy-start(f32[64,128]{1,0:T(8,128)} %param.17) | copy-start | bytes 98308
  755.9 18.6 %all-to-all-start.2 = ((f32[128,2,128]{2,1,0:T(2,128)}), f32[128,2,128]{2,1,0:T(2,128)S(1)}, u32[]{:S(2)}, u32[]{:S(2)}) async-start(f32[128,2,128]{2,1,0:T(2,128)} %select_select_fusion), calls=%async_computation.2 | async-start | bytes 262144 | tf_op jit(solution)/shard_map/all_to_all | solution.py:95
where the time goes:
time: 810 us
  local copies, waits for them, and re-layouts  603 us (74%)
  waiting for transfers between devices  117 us (14%)
  blocking collectives  31.1 us (4%)
  starting transfers between devices  26.4 us (3%)
  other arithmetic  24.4 us (3%)
    gather x1, local copies, waits for them, and re-layouts, local(): wanted = jnp.where(filled, jnp.take(home % per_opp, source), -1)  181 us
    gather x1, local copies, waits for them, and re-layouts, local(): served = jnp.take(policy, asked, axis=0).reshape(devices, limit, acts)  114 us
    all_to_all x1, waiting for transfers between devices, move_rows(): lax.all_to_all(blocks, GX_GY, split_axis=0, concat_axis=0, tiled=True)  99.3 us
    gather x1, local copies, waits for them, and re-layouts, local(): jnp.take(history_value, child_row.reshape(-1)).reshape(parents, acts)  90.5 us
    gather x1, local copies, waits for them, and re-layouts, local(): home = jnp.take(opp_home, opp_set)  90.5 us
    scatter x2, local copies, waits for them, and re-layouts, slot_source(): jnp.full((slots,), rows, jnp.int32).at[place]  61.3 us
    gather x1, local copies, waits for them, and re-layouts, local(): mine = jnp.take(fetched, place, axis=0)  59.4 us
    psum x4, blocking collectives, one_axis_at_a_time(): return functools.reduce(lax.psum, axes, value)  31.1 us
  transfers between devices with their start and end apart: 3, of which 3 were waited for; matrix products, arithmetic and copies ran while one was open for 0% of the time, Pallas kernels for 0%

commit v1 on v0

v1 whole, which is shorter than its diff:
```python
import functools

import jax
import jax.numpy as jnp
from jax import lax
from jax.experimental import pallas as pl
from jax.experimental.pallas import tpu as pltpu
from jax.sharding import Mesh
from jax.sharding import PartitionSpec as P

AXES = ("gx_0", "gx_1", "gy_0", "gy_1")
F32, BF16, I32 = jnp.float32, jnp.bfloat16, jnp.int32
NT = (((1,), (1,)), ((), ()))


def rows_iota(rows, cols):
    return lax.broadcasted_iota(I32, (rows, cols), 0)


def lanes_iota(rows, cols):
    return lax.broadcasted_iota(I32, (rows, cols), 1)


def dot(a, b):
    return jnp.dot(a, b, preferred_element_type=F32)


def one_hot_rows(rows, index):
    return (rows_iota(rows, index.shape[1]) == index).astype(F32).astype(BF16)


def pick(table, index, base=0):
    rows, n = table.shape
    mark = rows_iota(rows, n) == index
    return jnp.sum(jnp.where(mark, table, 0.0), axis=0, keepdims=True)


BLOCK = 8


def route_kernel(set_ref, home_ref, set2_ref, home2_ref,
                 want_ref, place_ref, want2_ref, place2_ref,
                 table, acc, carry):
    devices, slots = want_ref.shape
    home = home_ref[...]
    table[0:128, :] = ((home >> 9) - 256).astype(F32).T.astype(BF16)
    table[128:256, :] = ((home & 511) - 256).astype(F32).T.astype(BF16)
    acc[...] = jnp.zeros_like(acc)
    carry[...] = jnp.zeros_like(carry)
    upper = jnp.concatenate(
        [(rows_iota(128, 128) < lanes_iota(128, 128)).astype(F32), jnp.ones((128, 128), F32)], axis=1
    ).astype(BF16)

    def block(b, _):
        at = pl.ds(pl.multiple_of(b * BLOCK, BLOCK), BLOCK)
        index = set_ref[at, :]
        high, low = index >> 7, index & 127
        found = jnp.zeros((256, BLOCK * 128), F32)
        for c in range(table.shape[1] // 256):
            marks = jnp.concatenate(
                [one_hot_rows(256, high[j : j + 1, :] - 256 * c) for j in range(BLOCK)], axis=1
            )
            found += dot(table[:, 256 * c : 256 * (c + 1)], marks)
        members, values = [], []
        for j in range(BLOCK):
            lanes = slice(128 * j, 128 * (j + 1))
            mine = low[j : j + 1, :]
            top = pick(found[0:128, lanes], mine).astype(I32) + 256
            bottom = pick(found[128:256, lanes], mine).astype(I32) + 256
            row = (top << 9) + bottom
            owner, local = row >> 11, row & 2047
            member = rows_iota(128, 128) == owner
            member16 = member.astype(F32).astype(BF16)
            ahead = dot(member16, upper)
            rank = jnp.sum(
                jnp.where(member, ahead[:, :128] + carry[...], 0.0), axis=0, keepdims=True
            ).astype(I32)
            carry[...] += ahead[:, 128:]
            place_ref[pl.ds(b * BLOCK + j, 1), :] = owner * slots + rank
            mark = rows_iota(slots, 128) == rank
            values.append(
                jnp.concatenate(
                    [
                        jnp.where(mark, (local >> 6).astype(F32), 0.0),
                        jnp.where(mark, (local & 63).astype(F32), 0.0),
                    ],
                    axis=0,
                ).astype(BF16)
            )
            members.append(member16)
        acc[...] += lax.dot_general(
            jnp.concatenate(members, axis=1),
            jnp.concatenate(values, axis=1),
            NT,
            preferred_element_type=F32,
        )
        return 0

    lax.fori_loop(0, set_ref.shape[0] // BLOCK, block, 0)
    total = acc[...]
    want_ref[...] = (total[:, :slots] * 64.0 + total[:, slots:]).astype(I32)

    index2 = set2_ref[...]
    home2 = home2_ref[...]
    marks2 = one_hot_rows(home2.shape[0], index2 >> 7)
    top2 = dot((home2 >> 7).astype(F32).T.astype(BF16), marks2)
    bottom2 = dot((home2 & 127).astype(F32).T.astype(BF16), marks2)
    mine2 = index2 & 127
    row2 = pick(top2, mine2).astype(I32) * 128 + pick(bottom2, mine2).astype(I32)
    owner2, local2 = row2 >> 6, row2 & 63
    member2 = rows_iota(128, 128) == owner2
    ahead2 = dot(member2.astype(F32).astype(BF16), upper)
    rank2 = jnp.sum(jnp.where(member2, ahead2[:, :128], 0.0), axis=0, keepdims=True).astype(I32)
    place2_ref[...] = owner2 * 2 + rank2
    value2 = jnp.where(rows_iota(128, 128) == rank2, (local2 + 1).astype(F32), 0.0).astype(BF16)
    want2_ref[...] = lax.dot_general(
        member2.astype(F32).astype(BF16), value2, NT, preferred_element_type=F32
    ).astype(I32) - 1


def route(opp_set, opp_home, br_set, br_home, devices, slots):
    hist = opp_set.shape[0]
    return pl.pallas_call(
        route_kernel,
        out_shape=(
            jax.ShapeDtypeStruct((devices, slots), I32),
            jax.ShapeDtypeStruct((hist // 128, 128), I32),
            jax.ShapeDtypeStruct((devices, 128), I32),
            jax.ShapeDtypeStruct((1, 128), I32),
        ),
        scratch_shapes=[
            pltpu.VMEM((256, opp_home.shape[0] // 128), BF16),
            pltpu.VMEM((devices, 2 * slots), F32),
            pltpu.VMEM((devices, 128), F32),
        ],
        name="route",
    )(
        opp_set.reshape(-1, 128),
        opp_home.reshape(-1, 128),
        br_set.reshape(1, -1),
        br_home.reshape(-1, 128),
    )


def serve_kernel(asked_ref, cum_ref, out_ref, table):
    step = pl.program_id(0)
    half = table.shape[0]

    @pl.when(step == 0)
    def _():
        for part in range(2):
            cum = cum_ref[part * half : (part + 1) * half, :]
            policy = cum / jnp.sum(cum, axis=1, keepdims=True)
            table[:, 128 * part : 128 * (part + 1)] = policy.astype(BF16)

    for j in range(out_ref.shape[0]):
        device = step * out_ref.shape[0] + j
        column = jnp.sum(
            jnp.where(lanes_iota(*asked_ref.shape) == device, asked_ref[...], 0), axis=1, keepdims=True
        )
        slots = column.shape[0]
        row = column & (half - 1)
        marks = (lanes_iota(slots, half) == row).astype(F32).astype(BF16)
        both = dot(marks, table[...])
        out_ref[j] = jnp.where(column >= half, both[:, 128:], both[:, :128]).astype(BF16)


def serve(asked, opp_cum):
    devices, slots = asked.shape
    rows, acts = opp_cum.shape
    each = 8
    return pl.pallas_call(
        serve_kernel,
        grid=(devices // each,),
        in_specs=[
            pl.BlockSpec((slots, devices), lambda i: (0, 0)),
            pl.BlockSpec((rows, acts), lambda i: (0, 0)),
        ],
        out_specs=pl.BlockSpec((each, slots, acts), lambda i: (i, 0, 0)),
        out_shape=jax.ShapeDtypeStruct((devices, slots, acts), BF16),
        scratch_shapes=[pltpu.VMEM((rows // 2, 2 * acts), BF16)],
        name="serve",
    )(asked.T, opp_cum)


def arrange_kernel(place_ref, value_ref, out_ref, wide, slotted):
    hist = value_ref.shape[0]
    slotted[...] = jnp.zeros_like(slotted)
    wide[...] = value_ref[...].astype(F32)

    def some(b, _):
        for j in range(16):
            h = b * 16 + j
            slotted[pl.ds(place_ref[h], 1), :] = wide[pl.ds(h, 1), :]
        return 0

    lax.fori_loop(0, hist // 16, some, 0)
    out_ref[...] = slotted[...].astype(BF16)


def arrange(place, child_value, total):
    hist, acts = child_value.shape
    return pl.pallas_call(
        arrange_kernel,
        in_specs=[pl.BlockSpec(memory_space=pltpu.SMEM), pl.BlockSpec(memory_space=pltpu.VMEM)],
        out_shape=jax.ShapeDtypeStruct((total, acts), BF16),
        scratch_shapes=[pltpu.VMEM((hist, acts), F32), pltpu.VMEM((total, acts), F32)],
        cost_estimate=pl.CostEstimate(flops=0, transcendentals=0, bytes_accessed=200_000_000),
        name="arrange",
    )(place, child_value)


def split(x):
    high = x.astype(BF16)
    return high, (x - high.astype(F32)).astype(BF16)


def value_kernel(fetched_ref, child_ref, place_ref, next_ref, reach_ref, place2_ref,
                 value_ref, out_ref, table):
    step = pl.program_id(0)
    each, slots, acts = fetched_ref.shape

    @pl.when(step == 0)
    def _():
        table[...] = jnp.zeros_like(table)

    for j in range(each):
        product = fetched_ref[j].astype(F32) * child_ref[j].astype(F32)
        total = jnp.sum(product, axis=1, keepdims=True)
        table[...] = jnp.where(lanes_iota(slots, 128) == step * each + j, total, table[...])

    @pl.when(step == pl.num_programs(0) - 1)
    def _():
        pieces = jnp.concatenate(split(table[...]), axis=0)

        def history(b, _):
            at = pl.ds(pl.multiple_of(b * BLOCK, BLOCK), BLOCK)
            place = place_ref[at, :]
            owner, rank = place >> 8, place & 255
            marks = jnp.concatenate(
                [one_hot_rows(128, owner[j : j + 1, :]) for j in range(BLOCK)], axis=1
            )
            found = dot(pieces, marks)
            both = found[:slots, :] + found[slots:, :]
            for j in range(BLOCK):
                value_ref[pl.ds(b * BLOCK + j, 1), :] = pick(
                    both[:, 128 * j : 128 * (j + 1)], rank[j : j + 1, :]
                )
            return 0

        lax.fori_loop(0, place_ref.shape[0] // BLOCK, history, 0)
        values = jnp.concatenate(split(value_ref[...]), axis=0)

        def follow(b, _):
            at = pl.ds(pl.multiple_of(b * BLOCK, BLOCK), BLOCK)
            row = next_ref[at, :]
            marks = jnp.concatenate(
                [one_hot_rows(128, row[j : j + 1, :] & 127) for j in range(BLOCK)], axis=1
            )
            found = dot(values, marks)
            both = found[:128, :] + found[128:, :]
            for j in range(BLOCK):
                table[pl.ds(b * BLOCK + j, 1), :] = pick(
                    both[:, 128 * j : 128 * (j + 1)], row[j : j + 1, :] >> 7
                )
            return 0

        lax.fori_loop(0, next_ref.shape[0] // BLOCK, follow, 0)
        weighted = table[0:128, :] * reach_ref[...]
        marks2 = one_hot_rows(out_ref.shape[0], place2_ref[...])
        high, low = split(weighted)
        out_ref[...] = dot(marks2, high) + dot(marks2, low)


def values(fetched, arranged, place, child_row, reach, place2):
    devices, slots, acts = fetched.shape
    each = 8
    whole = lambda a: pl.BlockSpec(a.shape, lambda i: (0,) * a.ndim)
    block = pl.BlockSpec((each, slots, acts), lambda i: (i, 0, 0))
    rest = (place, child_row.reshape(-1, 128), reach.reshape(-1, 1), place2)
    return pl.pallas_call(
        value_kernel,
        grid=(devices // each,),
        in_specs=[block, block] + [whole(a) for a in rest],
        out_specs=(
            pl.BlockSpec(place.shape, lambda i: (0, 0)),
            pl.BlockSpec((2 * devices, acts), lambda i: (0, 0)),
        ),
        out_shape=(
            jax.ShapeDtypeStruct(place.shape, F32),
            jax.ShapeDtypeStruct((2 * devices, acts), F32),
        ),
        scratch_shapes=[pltpu.VMEM((slots, 128), F32)],
        name="values",
    )(fetched, arranged.reshape(fetched.shape), *rest)


def move(x):
    return lax.all_to_all(x, AXES, split_axis=0, concat_axis=0, tiled=True)


def local(child_value, child_row, opp_set, opp_home, opp_cum, reach, br_set, br_home, br_cum):
    devices = lax.axis_size(AXES)
    hist, acts = child_value.shape
    parents = reach.shape[0]
    slots = 2 * hist // devices
    want, place, want2, place2 = route(opp_set, opp_home, br_set, br_home, devices, slots)
    asked = move(jnp.concatenate([want, want2[:, :2]], axis=1))
    asked, asked2 = asked[:, :slots], asked[:, slots:].reshape(-1)
    served = serve(asked, opp_cum)
    fetched = move(served)
    arranged = arrange(place.reshape(-1), child_value, devices * slots)
    history_value, outgoing = values(fetched, arranged, place, child_row, reach, place2)
    incoming = move(outgoing.reshape(devices, 2, acts)).reshape(2 * devices, acts)
    member = (asked2[None, :] == jnp.arange(br_cum.shape[0], dtype=I32)[:, None]).astype(F32)
    action_value = jnp.dot(member, incoming, precision=lax.Precision.HIGHEST)
    br_policy = br_cum / jnp.sum(br_cum, axis=1, keepdims=True)
    regret_gap = jnp.max(action_value, axis=1) - jnp.sum(br_policy * action_value, axis=1)
    totals = functools.reduce(lax.psum, AXES, jnp.stack([jnp.sum(regret_gap), jnp.sum(reach)]))
    return history_value.reshape(-1), regret_gap, totals[0] / totals[1]


def solution(mesh):
    torus = Mesh(mesh.devices.reshape(4, 2, 4, 4), AXES)
    rows, flat = P(AXES, None), P(AXES)
    placed = (rows, rows, flat, P(), rows, flat, flat, P(), rows)
    return jax.shard_map(
        local, mesh=torus, in_specs=placed, out_specs=(flat, flat, P()), check_vma=False
    )
```

time: 810 us -> 277 us (0.34)
  local copies, waits for them, and re-layouts: 603 us -> 2.56 us
  Pallas kernels: 0 us -> 119 us
  waiting for transfers between devices: 117 us -> 82.1 us
  other arithmetic: 24.4 us -> 4.27 us
  blocking collectives: 31.1 us -> 49.6 us
  starting transfers between devices: 26.4 us -> 15 us
    gather x8 -> x0, local copies, waits for them, and re-layouts: 539 us -> none  [the longest x1 181 us: local(): wanted = jnp.where(filled, jnp.take(home % per_opp, source), -1)]
    pallas_call x0 -> x4, Pallas kernels: none -> 119 us  [the longest x1 33.8 us: route(): pl.pallas_call(route_kernel, out_shape=(jax.ShapeDtypeStruct((devices, sl...]
    scatter x2 -> x0, local copies, waits for them, and re-layouts: 61.3 us -> none  [slot_source(): jnp.full((slots,), rows, jnp.int32).at[place]]
    all_to_all x3 -> x2, waiting for transfers between devices: 117 us -> 82.1 us  [move(): return lax.all_to_all(x, AXES, split_axis=0, concat_axis=0, tiled=True)]
    all_to_all x0 -> x1, blocking collectives: none -> 21.2 us  [move(): return lax.all_to_all(x, AXES, split_axis=0, concat_axis=0, tiled=True)]
    all_to_all x3 -> x2, starting transfers between devices: 26.4 us -> 15 us  [move(): return lax.all_to_all(x, AXES, split_axis=0, concat_axis=0, tiled=True)]
    select_n x10 -> x0, other arithmetic: 10.8 us -> none  [the longest x1 7.61 us: local(): served = jnp.take(policy, asked, axis=0).reshape(devices, limit, acts)]
    dot_general x1 -> x0, other arithmetic: 8.21 us -> none  [local(): jnp.einsum('ra,ra->r', mine, child_value, preferred_element_type=jnp.floa...]
  transfers between devices with their start and end apart: 3 -> 2, of which waited for: 3 -> 2; matrix products, arithmetic and copies ran while one was open for 0% -> 1% of each run, Pallas kernels for 0% -> 9%
where the time goes in v1:
time: 277 us; the launch traced here: 276 us
  Pallas kernels  119 us (43%)
  waiting for transfers between devices  82.1 us (30%)
  blocking collectives  49.6 us (18%)
  starting transfers between devices  15 us (5%)
  other arithmetic  4.27 us (2%)
  between operations  3.2 us (1%)
    all_to_all x2, waiting for transfers between devices, move(): return lax.all_to_all(x, AXES, split_axis=0, concat_axis=0, tiled=True)  82.1 us
    pallas_call x1, Pallas kernels, route(): pl.pallas_call(route_kernel, out_shape=(jax.ShapeDtypeStruct((devices, sl...  33.8 us
    pallas_call x1, Pallas kernels, serve(): pl.pallas_call(serve_kernel, grid=(devices // each,), in_specs=[pl.BlockS...  33.8 us
    psum x4, blocking collectives, local(): functools.reduce(lax.psum, AXES, jnp.stack([jnp.sum(regret_gap), jnp.sum(...  28.4 us
    pallas_call x1, Pallas kernels, values(): pl.pallas_call(value_kernel, grid=(devices // each,), in_specs=[block, bl...  26 us
    pallas_call x1, Pallas kernels, arrange(): pl.pallas_call(arrange_kernel, in_specs=[pl.BlockSpec(memory_space=pltpu....  25.6 us
    all_to_all x1, blocking collectives, move(): return lax.all_to_all(x, AXES, split_axis=0, concat_axis=0, tiled=True)  21.2 us
    all_to_all x2, starting transfers between devices, move(): return lax.all_to_all(x, AXES, split_axis=0, concat_axis=0, tiled=True)  15 us
  transfers between devices with their start and end apart: 2, of which 2 were waited for; matrix products, arithmetic and copies ran while one was open for 1% of the time, Pallas kernels for 9%

profile of v1, /device:TPU:0, one launch (start us, length us, event | category | flops | bytes accessed | tf_op | source)
XLA Modules:
  0.0 276.2 jit_solution(9516867697866202060)
XLA Ops:
  0.6 33.8 %route.1 = (s32[128,256]{1,0:T(8,128)}, s32[128,128]{1,0:T(8,128)}, s32[128,128]{1,0:T(8,128)}, s32[1,128]{1,0:T(1,128)}) custom-call(s32[128,128]{1,0:T(8,128)} %bitcast.29, s32[2048,128]{1,0:T(8,128)} %bitcast.22, s32[1,128]{1,0:T(1,128)} %bitcast.32, s32[64,128]{1,0:T(8,128)} %bitcast.31), custom_call_target="tpu_custom_call" | custom-call | tf_op jit(solution)/shard_map/route/pallas_call | solution.py:123
  34.4 1.0 add_bitcast_fusion
  35.4 0.2 copy.19
  35.6 21.2 %all_to_all.22 = s32[128,1,258]{2,1,0:T(1,128)S(1)} all-to-all(s32[128,1,258]{2,1,0:T(1,128)S(1)} %copy.19), channel_id=1, replica_groups=mesh['gx_0'=4,'gx_1'=2,'gy_0'=4,'gy_1'=4] {'gx_0','gx_1','gy_0','gy_1'}, dimensions={0} | all-to-all | bytes 264192 | tf_op jit(solution)/shard_map/all_to_all | solution.py:299
  56.8 0.1 copy.20
  56.9 0.7 slice_bitcast_fusion.asked_ref
  57.6 33.8 %serve.1 = bf16[128,256,128]{2,1,0:T(8,128)(2,1)} custom-call(s32[256,128]{1,0:T(8,128)} %slice_bitcast_fusion.asked_ref, f32[2048,128]{1,0:T(8,128)} %cum_ref.1), custom_call_target="tpu_custom_call" | custom-call | tf_op jit(solution)/shard_map/serve/pallas_call | solution.py:172
  91.3 0.0 copy-start.1
  91.3 6.1 %all-to-all-start.1 = ((bf16[128,256,128]{2,1,0:T(8,128)(2,1)}), bf16[128,256,128]{2,1,0:T(8,128)(2,1)}, u32[]{:S(2)}, u32[]{:S(2)}) async-start(bf16[128,256,128]{2,1,0:T(8,128)(2,1)} %serve.1), calls=%async_computation.1 | async-start | bytes 16777216 | tf_op jit(solution)/shard_map/all_to_all | solution.py:299
  97.4 0.0 copy-done.1
  97.4 0.7 copy.21.reach_ref
  98.1 25.6 %arrange.1 = bf16[32768,128]{1,0:T(8,128)(2,1)} custom-call(s32[16384]{0:T(1024)} %bitcast.25, bf16[16384,128]{1,0:T(8,128)(2,1)} %value_ref.1), custom_call_target="tpu_custom_call" | custom-call | bytes 200000000 | tf_op jit(solution)/shard_map/arrange/pallas_call | solution.py:203
  123.7 73.6 %all-to-all-done.1.fetched_ref = bf16[128,256,128]{2,1,0:T(8,128)(2,1)} async-done(((bf16[128,256,128]{2,1,0:T(8,128)(2,1)}), bf16[128,256,128]{2,1,0:T(8,128)(2,1)}, u32[]{:S(2)}, u32[]{:S(2)}) %all-to-all-start.1) | async-done | bytes 8388640 | tf_op jit(solution)/shard_map/all_to_all | solution.py:299
  197.3 0.0 copy-start
  197.3 26.0 %values.1 = (f32[128,128]{1,0:T(8,128)}, f32[256,128]{1,0:T(8,128)}) custom-call(bf16[128,256,128]{2,1,0:T(8,128)(2,1)} %all-to-all-done.1.fetched_ref, bf16[128,256,128]{2,1,0:T(8,128)(2,1)} %bitcast.21, s32[128,128]{1,0:T(8,128)} %get-tuple-element.11.place_ref, s32[128,128]{1,0:T(8,128)} %bitcast.28, f32[128,1]{1,0:T(8,128)} %copy.21.reach_ref, ...), custom_call_target="tpu_custom_call" | custom-call | tf_op jit(solution)/shard_map/values/pallas_call | solution.py:281
  223.3 8.9 %all-to-all-start.2 = ((f32[128,2,128]{2,1,0:T(2,128)}), f32[128,2,128]{2,1,0:T(2,128)S(1)}, u32[]{:S(2)}, u32[]{:S(2)}) async-start(f32[128,2,128]{2,1,0:T(2,128)} %bitcast.26), calls=%async_computation.2 | async-start | bytes 262144 | tf_op jit(solution)/shard_map/all_to_all | solution.py:299
  232.3 0.7 reduce_sum.39
  233.0 0.0 copy-done
  233.0 0.1 reduce_sum.36
  233.1 0.1 copy.22
  233.2 0.1 eq.15
  233.4 8.5 %all-to-all-done.2 = f32[128,2,128]{2,1,0:T(2,128)S(1)} async-done(((f32[128,2,128]{2,1,0:T(2,128)}), f32[128,2,128]{2,1,0:T(2,128)S(1)}, u32[]{:S(2)}, u32[]{:S(2)}) %all-to-all-start.2) | async-done | bytes 131104 | tf_op jit(solution)/shard_map/all_to_all | solution.py:299
  241.9 0.3 multiply_reduce_fusion
  242.2 1.1 fusion.2
  243.3 1.4 pad_maximum_fusion
  244.7 8.8 %psum.28 = f32[2]{0:T(128)S(1)} all-reduce(f32[2]{0:T(128)S(1)} %pad_maximum_fusion), channel_id=1, replica_groups=mesh['gx_0'=4,'gx_1'=2,'gy_0'=4,'gy_1'=4] {'gx_0'}, use_global_device_ids=true, to_apply=%region_5.0 | all-reduce | flops 2 | bytes 16 | tf_op jit(solution)/shard_map/psum | solution.py:319
  253.5 2.5 psum.29
  255.9 8.3 %psum.30 = f32[2]{0:T(128)S(1)} all-reduce(f32[2]{0:T(128)S(1)} %psum.29), channel_id=1, replica_groups=mesh['gx_0'=4,'gx_1'=2,'gy_0'=4,'gy_1'=4] {'gy_0'}, use_global_device_ids=true, to_apply=%region_7.0 | all-reduce | flops 2 | bytes 16 | tf_op jit(solution)/shard_map/psum | solution.py:319
  264.3 8.8 %psum.31 = f32[2]{0:T(128)S(1)} all-reduce(f32[2]{0:T(128)S(1)} %psum.30), channel_id=1, replica_groups=mesh['gx_0'=4,'gx_1'=2,'gy_0'=4,'gy_1'=4] {'gy_1'}, use_global_device_ids=true, to_apply=%region_8.0 | all-reduce | flops 2 | bytes 16 | tf_op jit(solution)/shard_map/psum | solution.py:319
  273.1 0.6 fusion.3
  (1 shorter events, 0.0 us)
Async XLA Ops:
  91.3 6.1 %copy-start.1 = (f32[128]{0:T(128)S(1)}, f32[128]{0:T(128)}, u32[]{:S(2)}) copy-start(f32[128]{0:T(128)} %param.14) | copy-start | bytes 1540
  91.3 106.0 %all-to-all-start.1 = ((bf16[128,256,128]{2,1,0:T(8,128)(2,1)}), bf16[128,256,128]{2,1,0:T(8,128)(2,1)}, u32[]{:S(2)}, u32[]{:S(2)}) async-start(bf16[128,256,128]{2,1,0:T(8,128)(2,1)} %serve.1), calls=%async_computation.1 | async-start | bytes 16777216 | tf_op jit(solution)/shard_map/all_to_all | solution.py:299
  197.3 35.7 %copy-start = (f32[64,128]{1,0:T(8,128)S(1)}, f32[64,128]{1,0:T(8,128)}, u32[]{:S(2)}) copy-start(f32[64,128]{1,0:T(8,128)} %param.17) | copy-start | bytes 98308
  223.3 18.5 %all-to-all-start.2 = ((f32[128,2,128]{2,1,0:T(2,128)}), f32[128,2,128]{2,1,0:T(2,128)S(1)}, u32[]{:S(2)}, u32[]{:S(2)}) async-start(f32[128,2,128]{2,1,0:T(2,128)} %bitcast.26), calls=%async_computation.2 | async-start | bytes 262144 | tf_op jit(solution)/shard_map/all_to_all | solution.py:299

commit v2 on v1

v2 whole, which is shorter than its diff:
```python
import functools

import jax
import jax.numpy as jnp
from jax import lax
from jax.experimental import pallas as pl
from jax.experimental.pallas import tpu as pltpu
from jax.sharding import Mesh
from jax.sharding import PartitionSpec as P

AXES = ("gx_0", "gx_1", "gy_0", "gy_1")
F32, BF16, I32 = jnp.float32, jnp.bfloat16, jnp.int32
NT = (((1,), (1,)), ((), ()))


def rows_iota(rows, cols):
    return lax.broadcasted_iota(I32, (rows, cols), 0)


def lanes_iota(rows, cols):
    return lax.broadcasted_iota(I32, (rows, cols), 1)


def dot(a, b):
    return jnp.dot(a, b, preferred_element_type=F32)


def one_hot_rows(rows, index):
    return (rows_iota(rows, index.shape[1]) == index).astype(F32).astype(BF16)


def pick(table, index, base=0):
    rows, n = table.shape
    mark = rows_iota(rows, n) == index
    return jnp.sum(jnp.where(mark, table, 0.0), axis=0, keepdims=True)


BLOCK = 8


def route_kernel(set_ref, home_ref, set2_ref, home2_ref,
                 want_ref, source_ref, place_ref, place2_ref,
                 table, acc, carry):
    devices, slots = want_ref.shape
    home = home_ref[...]
    table[0:128, :] = ((home >> 9) - 256).astype(F32).T.astype(BF16)
    table[128:256, :] = ((home & 511) - 256).astype(F32).T.astype(BF16)
    acc[...] = jnp.zeros_like(acc)
    carry[...] = jnp.zeros_like(carry)
    upper = jnp.concatenate(
        [(rows_iota(128, 128) < lanes_iota(128, 128)).astype(F32), jnp.ones((128, 128), F32)], axis=1
    ).astype(BF16)

    def block(b, _):
        at = pl.ds(pl.multiple_of(b * BLOCK, BLOCK), BLOCK)
        index = set_ref[at, :]
        high, low = index >> 7, index & 127
        found = jnp.zeros((256, BLOCK * 128), F32)
        for c in range(table.shape[1] // 256):
            marks = jnp.concatenate(
                [one_hot_rows(256, high[j : j + 1, :] - 256 * c) for j in range(BLOCK)], axis=1
            )
            found += dot(table[:, 256 * c : 256 * (c + 1)], marks)
        members, values = [], []
        for j in range(BLOCK):
            lanes = slice(128 * j, 128 * (j + 1))
            mine = low[j : j + 1, :]
            top = pick(found[0:128, lanes], mine).astype(I32) + 256
            bottom = pick(found[128:256, lanes], mine).astype(I32) + 256
            row = (top << 9) + bottom
            owner, local = row >> 11, row & 2047
            member = rows_iota(128, 128) == owner
            member16 = member.astype(F32).astype(BF16)
            ahead = dot(member16, upper)
            rank = jnp.sum(
                jnp.where(member, ahead[:, :128] + carry[...], 0.0), axis=0, keepdims=True
            ).astype(I32)
            carry[...] += ahead[:, 128:]
            place_ref[pl.ds(b * BLOCK + j, 1), :] = owner * slots + rank
            mark = rows_iota(slots, 128) == rank
            lane = lanes_iota(1, 128).astype(F32)
            values.append(
                jnp.concatenate(
                    [
                        jnp.where(mark, (local >> 6).astype(F32), 0.0),
                        jnp.where(mark, (local & 63).astype(F32), 0.0),
                        jnp.where(mark, (b * BLOCK + j).astype(F32), 0.0),
                        jnp.where(mark, lane, 0.0),
                    ],
                    axis=0,
                ).astype(BF16)
            )
            members.append(member16)
        acc[...] += lax.dot_general(
            jnp.concatenate(members, axis=1),
            jnp.concatenate(values, axis=1),
            NT,
            preferred_element_type=F32,
        )
        return 0

    lax.fori_loop(0, set_ref.shape[0] // BLOCK, block, 0)
    total = acc[...]
    local = total[:, :slots] * 64.0 + total[:, slots : 2 * slots]
    source = total[:, 2 * slots : 3 * slots] * 128.0 + total[:, 3 * slots :]
    source_ref[...] = source.astype(I32)

    index2 = set2_ref[...]
    home2 = home2_ref[...]
    marks2 = one_hot_rows(home2.shape[0], index2 >> 7)
    top2 = dot((home2 >> 7).astype(F32).T.astype(BF16), marks2)
    bottom2 = dot((home2 & 127).astype(F32).T.astype(BF16), marks2)
    mine2 = index2 & 127
    row2 = pick(top2, mine2).astype(I32) * 128 + pick(bottom2, mine2).astype(I32)
    owner2, local2 = row2 >> 6, row2 & 63
    member2 = rows_iota(128, 128) == owner2
    ahead2 = dot(member2.astype(F32).astype(BF16), upper)
    rank2 = jnp.sum(jnp.where(member2, ahead2[:, :128], 0.0), axis=0, keepdims=True).astype(I32)
    place2_ref[...] = owner2 * 2 + rank2
    value2 = jnp.where(rows_iota(slots, 128) == rank2, (local2 + 1).astype(F32), 0.0).astype(BF16)
    extra = lax.dot_general(
        member2.astype(F32).astype(BF16), value2, NT, preferred_element_type=F32
    )
    want_ref[...] = (local + 2048.0 * extra).astype(I32)


def route(opp_set, opp_home, br_set, br_home, devices, slots):
    hist = opp_set.shape[0]
    return pl.pallas_call(
        route_kernel,
        out_shape=(
            jax.ShapeDtypeStruct((devices, slots), I32),
            jax.ShapeDtypeStruct((devices, slots), I32),
            jax.ShapeDtypeStruct((hist // 128, 128), I32),
            jax.ShapeDtypeStruct((1, 128), I32),
        ),
        scratch_shapes=[
            pltpu.VMEM((256, opp_home.shape[0] // 128), BF16),
            pltpu.VMEM((devices, 4 * slots), F32),
            pltpu.VMEM((devices, 128), F32),
        ],
        name="route",
    )(
        opp_set.reshape(-1, 128),
        opp_home.reshape(-1, 128),
        br_set.reshape(1, -1),
        br_home.reshape(-1, 128),
    )


def split(x):
    high = x.astype(BF16)
    return high, (x - high.astype(F32)).astype(BF16)


def find(pieces, rows, index, high_of, low_of):
    marks = jnp.concatenate(
        [one_hot_rows(rows, high_of(index[j : j + 1, :])) for j in range(BLOCK)], axis=1
    )
    found = dot(pieces, marks)
    half = found.shape[0] // 2
    both = found[:half, :] + found[half:, :]
    return [
        pick(both[:, 128 * j : 128 * (j + 1)], low_of(index[j : j + 1, :])) for j in range(BLOCK)
    ]


def look_up(pieces, rows, index_ref, out_ref, high_of, low_of, cast=lambda x: x):
    def block(b, _):
        at = pl.ds(pl.multiple_of(b * BLOCK, BLOCK), BLOCK)
        for j, row in enumerate(find(pieces, rows, index_ref[at, :], high_of, low_of)):
            out_ref[pl.ds(b * BLOCK + j, 1), :] = cast(row)
        return 0

    lax.fori_loop(0, index_ref.shape[0] // BLOCK, block, 0)


def exchange_kernel(sizes, source_ref, want_ref, place_ref, next_ref, place2_ref, reach_ref,
                    cum_ref, br_ref, child_ref,
                    value_ref, gap_ref, total_ref,
                    asked, columns, table, wide, send, recv, gathered, sums, jump,
                    outgoing, incoming, part, parts,
                    ask_out, ask_in, row_out, row_in, act_out, act_in, sum_out, sum_in):
    devices, slots, acts = send.shape
    me = [lax.axis_index(a) for a in AXES]

    def number(c):
        return ((c[0] * sizes[1] + c[1]) * sizes[2] + c[2]) * sizes[3] + c[3]

    my = number(me)

    def shift(i):
        q, s = i // 2, 2 * (i % 2)
        return q % 4 + s, (q // 32 + i) % 2, (q + q // 4) % 4 + s, (q + q // 16) % 2 + s

    def to(i):
        c = tuple((m + d) % n for m, d, n in zip(me, shift(i), sizes))
        return c, number(c)

    def back(i):
        return number(tuple((m + 2 * n - d) % n for m, d, n in zip(me, shift(i), sizes)))

    def copy(src, dst, out_sem, in_sem, device):
        return pltpu.make_async_remote_copy(
            src_ref=src, dst_ref=dst, send_sem=out_sem, recv_sem=in_sem,
            device_id=device, device_id_type=pl.DeviceIdType.MESH,
        )

    def each(body, first=1):
        lax.fori_loop(first, devices, lambda i, c: (body(i), c)[1], 0)

    barrier = pltpu.get_barrier_semaphore()
    each(lambda i: pl.semaphore_signal(
        barrier, inc=1, device_id=to(i)[0], device_id_type=pl.DeviceIdType.MESH))
    rows = table.shape[0]
    for p in range(4):
        cum = cum_ref[p * rows : (p + 1) * rows, :]
        policy = cum / jnp.sum(cum, axis=1, keepdims=True)
        table[:, 128 * p : 128 * (p + 1)] = policy.astype(BF16)
    pl.semaphore_wait(barrier, devices - 1)

    def request(i):
        device, n = to(i)
        copy(want_ref.at[n], asked.at[my], ask_out, ask_in, device).start()

    each(request)
    asked[my] = want_ref[my]
    wide[...] = child_ref[...].astype(F32)
    most = pl.ds(0, devices - 1)
    copy(want_ref.at[most], asked.at[most], ask_out, ask_in, tuple(me)).wait()
    for p in range(2):
        columns[128 * p : 128 * (p + 1), :] = asked[:, p, :].astype(F32).T.astype(I32)

    def served(n):
        column = jnp.sum(
            jnp.where(lanes_iota(slots, devices) == n, columns[...], 0), axis=1, keepdims=True
        ) & (4 * rows - 1)
        marks = (lanes_iota(slots, rows) == (column & (rows - 1))).astype(F32).astype(BF16)
        found = dot(marks, table[...])
        which = column // rows
        out = found[:, 384:]
        for p in range(3):
            out = jnp.where(which == p, found[:, 128 * p : 128 * (p + 1)], out)
        return out.astype(BF16)

    def launch(i):
        device, n = to(i)
        copy(send.at[n], recv.at[my], row_out, row_in.at[my], device).start()

    def serve(i):
        send[to(i)[1]] = served(to(i)[1])

        @pl.when(i > 1)
        def _():
            launch(i - 1)

    each(serve)
    launch(jnp.int32(devices - 1))
    recv[my] = served(my)

    places = place_ref[...]
    look_up(
        jnp.concatenate(
            [((places >> 8) * 256).astype(F32).astype(BF16), (places & 255).astype(F32).astype(BF16)],
            axis=0,
        ),
        128, next_ref, jump, lambda x: x & 127, lambda x: x >> 7, lambda x: x.astype(I32),
    )

    def consume(n):
        def some(g, _):
            for q in range(16):
                k = g * 16 + q
                gathered[pl.ds(k, 1), :] = wide[pl.ds(source_ref[n * slots + k], 1), :]
            return 0

        lax.fori_loop(0, slots // 16, some, 0)

    def finish(n):
        product = recv[n].astype(F32) * gathered[...]
        total = jnp.sum(product, axis=1, keepdims=True)
        sums[...] = jnp.where(lanes_iota(slots, devices) == n, total, sums[...])

    sums[...] = jnp.zeros_like(sums)
    consume(my)
    finish(my)

    def take(i):
        n = back(i)
        consume(n)
        copy(send.at[n], recv.at[n], row_out, row_in.at[n], tuple(me)).wait_recv()
        finish(n)

    each(take)
    pieces = jnp.concatenate(split(sums[...]), axis=0)
    look_up(pieces, 128, jump, part, lambda x: x >> 8, lambda x: x & 255)
    weighted = part[...] * reach_ref[...]
    high, low = split(weighted)
    for s in range(2):
        marks = (rows_iota(devices, 128) * 2 + s == place2_ref[...]).astype(F32).astype(BF16)
        outgoing[:, s, :] = dot(marks, high) + dot(marks, low)

    def act(i):
        device, n = to(i)
        copy(outgoing.at[n], incoming.at[my], act_out, act_in, device).start()

    each(act)
    incoming[my] = outgoing[my]
    look_up(pieces, 128, place_ref, value_ref, lambda x: x >> 8, lambda x: x & 255)
    copy(outgoing.at[most], incoming.at[most], act_out, act_in, tuple(me)).wait()
    action = jnp.zeros((br_ref.shape[0], acts), F32)
    for s in range(2):
        owned = columns[s : s + 1, :] >> 11
        member = (rows_iota(br_ref.shape[0], devices) + 1 == owned).astype(F32).astype(BF16)
        high, low = split(incoming[:, s, :])
        action += dot(member, high) + dot(member, low)
    br = br_ref[...]
    br_policy = br / jnp.sum(br, axis=1, keepdims=True)
    gap = jnp.max(action, axis=1, keepdims=True) - jnp.sum(br_policy * action, axis=1, keepdims=True)
    across = jnp.where(rows_iota(gap.shape[0], 128) == lanes_iota(gap.shape[0], 128), gap, 0.0)
    gap_row = jnp.sum(across, axis=0, keepdims=True)
    gap_ref[...] = gap_row[:, : gap_ref.shape[1]]
    lane = lanes_iota(1, 128)
    both = jnp.where(
        lane == 0,
        jnp.sum(gap_row, axis=1, keepdims=True),
        jnp.where(lane == 1, jnp.sum(reach_ref[...], axis=0, keepdims=True), 0.0),
    )
    parts[my] = both
    total_ref[...] = both

    def tell(i):
        device, n = to(i)
        copy(total_ref, parts.at[my], sum_out, sum_in, device).start()

    each(tell)
    copy(parts.at[most], parts.at[most], sum_out, sum_in, tuple(me)).wait()
    total = jnp.sum(parts[:, 0, :], axis=0, keepdims=True)
    top = jnp.sum(jnp.where(lane == 0, total, 0.0), axis=1, keepdims=True)
    bottom = jnp.sum(jnp.where(lane == 1, total, 0.0), axis=1, keepdims=True)
    total_ref[...] = jnp.broadcast_to(top / bottom, (1, 128))
    copy(send.at[most], recv.at[most], row_out, row_in.at[0], tuple(me)).wait_send()


def exchange(sizes, source, want, place, child_row, place2, reach, opp_cum, br_cum, child_value):
    devices, slots = want.shape
    hist, acts = child_value.shape
    rows = opp_cum.shape[0] // 4
    vmem, smem = pl.BlockSpec(memory_space=pltpu.VMEM), pl.BlockSpec(memory_space=pltpu.SMEM)
    dma = pltpu.SemaphoreType.DMA
    return pl.pallas_call(
        functools.partial(exchange_kernel, sizes),
        in_specs=[smem] + [vmem] * 8,
        out_specs=[vmem] * 3,
        out_shape=(
            jax.ShapeDtypeStruct((hist // 128, 128), F32),
            jax.ShapeDtypeStruct((1, br_cum.shape[0]), F32),
            jax.ShapeDtypeStruct((1, 128), F32),
        ),
        scratch_shapes=[
            pltpu.VMEM((devices, 2, 128), I32),
            pltpu.VMEM((slots, devices), I32),
            pltpu.VMEM((rows, 4 * acts), BF16),
            pltpu.VMEM((hist, acts), F32),
            pltpu.VMEM((devices, slots, acts), BF16),
            pltpu.VMEM((devices, slots, acts), BF16),
            pltpu.VMEM((slots, acts), F32),
            pltpu.VMEM((slots, devices), F32),
            pltpu.VMEM((128, 128), I32),
            pltpu.VMEM((devices, 2, acts), F32),
            pltpu.VMEM((devices, 2, acts), F32),
            pltpu.VMEM((128, 128), F32),
            pltpu.VMEM((devices, 1, 128), F32),
            dma, dma, dma, dma((devices,)), dma, dma, dma, dma,
        ],
        compiler_params=pltpu.CompilerParams(collective_id=0, has_side_effects=True),
        name="exchange",
    )(
        source.reshape(-1),
        want.reshape(devices, 2, 128),
        place,
        child_row.reshape(-1, 128),
        place2,
        reach.reshape(-1, 1),
        opp_cum,
        br_cum,
        child_value,
    )


def local(child_value, child_row, opp_set, opp_home, opp_cum, reach, br_set, br_home, br_cum):
    sizes = tuple(lax.axis_size(a) for a in AXES)
    devices = lax.axis_size(AXES)
    slots = 2 * child_value.shape[0] // devices
    want, source, place, place2 = route(opp_set, opp_home, br_set, br_home, devices, slots)
    history_value, gap, ratio = exchange(
        sizes, source, want, place, child_row, place2, reach, opp_cum, br_cum, child_value
    )
    return history_value.reshape(-1), gap.reshape(-1), ratio[0, 0]


def solution(mesh):
    torus = Mesh(mesh.devices.reshape(4, 2, 4, 4), AXES)
    rows, flat = P(AXES, None), P(AXES)
    placed = (rows, rows, flat, P(), rows, flat, flat, P(), rows)
    return jax.shard_map(
        local, mesh=torus, in_specs=placed, out_specs=(flat, flat, P()), check_vma=False
    )
```

time: 277 us -> 238 us (0.86)
  Pallas kernels: 119 us -> 228 us
  waiting for transfers between devices: 82.1 us -> 0 us
  blocking collectives: 49.6 us -> 0 us
  starting transfers between devices: 15 us -> 0 us
  local copies, waits for them, and re-layouts: 2.56 us -> 7.27 us
  other arithmetic: 4.27 us -> 0 us
    pallas_call x3 -> x1, Pallas kernels: 85.4 us -> 189 us  [exchange(): pl.pallas_call(functools.partial(exchange_kernel, sizes), in_specs=[smem]...]
    all_to_all x2 -> x0, waiting for transfers between devices: 82.1 us -> none  [move(): return lax.all_to_all(x, AXES, split_axis=0, concat_axis=0, tiled=True)]
    psum x4 -> x0, blocking collectives: 28.4 us -> none  [local(): functools.reduce(lax.psum, AXES, jnp.stack([jnp.sum(regret_gap), jnp.sum(...]
    all_to_all x1 -> x0, blocking collectives: 21.2 us -> none  [move(): return lax.all_to_all(x, AXES, split_axis=0, concat_axis=0, tiled=True)]
    all_to_all x2 -> x0, starting transfers between devices: 15 us -> none  [move(): return lax.all_to_all(x, AXES, split_axis=0, concat_axis=0, tiled=True)]
    pallas_call x1, Pallas kernels: 33.8 us -> 39.3 us  [route(): pl.pallas_call(route_kernel, out_shape=(jax.ShapeDtypeStruct((devices, sl...]
    unnamed x4 -> x3, local copies, waits for them, and re-layouts: 0.01 us -> 4.27 us
  transfers between devices with their start and end apart: 2 -> 0, of which waited for: 2 -> 0; matrix products, arithmetic and copies ran while one was open for 1% -> 0% of each run, Pallas kernels for 9% -> 0%
where the time goes in v2:
time: 238 us
  Pallas kernels  228 us (96%)
  local copies, waits for them, and re-layouts  7.27 us (3%)
    pallas_call x1, Pallas kernels, exchange(): pl.pallas_call(functools.partial(exchange_kernel, sizes), in_specs=[smem]...  189 us
    pallas_call x1, Pallas kernels, route(): pl.pallas_call(route_kernel, out_shape=(jax.ShapeDtypeStruct((devices, sl...  39.3 us

profile of v2, /device:TPU:0, one launch (start us, length us, event | category | flops | bytes accessed | tf_op | source)
XLA Modules:
  0.0 237.8 jit_solution(2676672805056400815)
XLA Ops:
  0.6 39.3 %route.1 = (s32[128,256]{1,0:T(8,128)}, s32[128,256]{1,0:T(8,128)}, s32[128,128]{1,0:T(8,128)}, s32[1,128]{1,0:T(1,128)}) custom-call(s32[128,128]{1,0:T(8,128)} %bitcast.16, s32[2048,128]{1,0:T(8,128)} %bitcast.12, s32[1,128]{1,0:T(1,128)} %bitcast.19, s32[64,128]{1,0:T(8,128)} %bitcast.18), custom_call_target="tpu_custom_call" | custom-call | tf_op jit(solution)/shard_map/route/pallas_call | solution.py:129
  39.9 1.6 copy.13
  41.5 1.6 reshape.41.want_ref
  43.1 1.4 copy.12.reach_ref
  44.5 188.9 %exchange.1 = (f32[128,128]{1,0:T(8,128)}, f32[1,64]{1,0:T(1,128)}, f32[1,128]{1,0:T(1,128)}) custom-call(s32[32768]{0:T(1024)} %bitcast.13, s32[128,2,128]{2,1,0:T(2,128)} %reshape.41.want_ref, s32[128,128]{1,0:T(8,128)} %get-tuple-element.12.place_ref, s32[128,128]{1,0:T(8,128)} %bitcast.15, s32[1,128]{1,0:T(1,128)} %get-tuple-element.13.place2_ref, ...), custom_call_target="tpu_custom_call" | custom-call | tf_op jit(solution)/shard_map/exchange/pallas_call | solution.py:351
  233.4 1.5 copy.17
  234.9 1.2 copy.18

commit v3 on v2

--- a/solution.py
+++ b/solution.py
@@ -41,10 +41,14 @@
 def route_kernel(set_ref, home_ref, set2_ref, home2_ref,
                  want_ref, source_ref, place_ref, place2_ref,
                  table, acc, carry):
-    devices, slots = want_ref.shape
-    home = home_ref[...]
-    table[0:128, :] = ((home >> 9) - 256).astype(F32).T.astype(BF16)
-    table[128:256, :] = ((home & 511) - 256).astype(F32).T.astype(BF16)
+    devices, slots = want_ref.shape[0], 256
+    wide = table.shape[1]
+    for q in range(4):
+        home = home_ref[pl.ds(q, wide, stride=4), :]
+        table[128 * q : 128 * (q + 1), :] = ((home >> 9) - 256).astype(F32).T.astype(BF16)
+        table[512 + 128 * q : 512 + 128 * (q + 1), :] = (
+            ((home & 511) - 256).astype(F32).T.astype(BF16)
+        )
     acc[...] = jnp.zeros_like(acc)
     carry[...] = jnp.zeros_like(carry)
     upper = jnp.concatenate(
@@ -54,19 +58,17 @@
     def block(b, _):
         at = pl.ds(pl.multiple_of(b * BLOCK, BLOCK), BLOCK)
         index = set_ref[at, :]
-        high, low = index >> 7, index & 127
-        found = jnp.zeros((256, BLOCK * 128), F32)
-        for c in range(table.shape[1] // 256):
-            marks = jnp.concatenate(
-                [one_hot_rows(256, high[j : j + 1, :] - 256 * c) for j in range(BLOCK)], axis=1
-            )
-            found += dot(table[:, 256 * c : 256 * (c + 1)], marks)
+        high, low = index >> 9, index & 511
+        marks = jnp.concatenate(
+            [one_hot_rows(wide, high[j : j + 1, :]) for j in range(BLOCK)], axis=1
+        )
+        found = dot(table[...], marks)
         members, values = [], []
         for j in range(BLOCK):
             lanes = slice(128 * j, 128 * (j + 1))
             mine = low[j : j + 1, :]
-            top = pick(found[0:128, lanes], mine).astype(I32) + 256
-            bottom = pick(found[128:256, lanes], mine).astype(I32) + 256
+            top = pick(found[0:512, lanes], mine).astype(I32) + 256
+            bottom = pick(found[512:1024, lanes], mine).astype(I32) + 256
             row = (top << 9) + bottom
             owner, local = row >> 11, row & 2047
             member = rows_iota(128, 128) == owner
@@ -78,14 +80,12 @@
             carry[...] += ahead[:, 128:]
             place_ref[pl.ds(b * BLOCK + j, 1), :] = owner * slots + rank
             mark = rows_iota(slots, 128) == rank
-            lane = lanes_iota(1, 128).astype(F32)
+            code = ((b * BLOCK + j) * 128 + lanes_iota(1, 128)) * 2048 + local
             values.append(
                 jnp.concatenate(
                     [
-                        jnp.where(mark, (local >> 6).astype(F32), 0.0),
-                        jnp.where(mark, (local & 63).astype(F32), 0.0),
-                        jnp.where(mark, (b * BLOCK + j).astype(F32), 0.0),
-                        jnp.where(mark, lane, 0.0),
+                        jnp.where(mark, piece.astype(F32), 0.0)
+                        for piece in (code >> 18, ((code >> 9) & 511) - 256, (code & 511) - 256)
                     ],
                     axis=0,
                 ).astype(BF16)
@@ -101,10 +101,13 @@
 
     lax.fori_loop(0, set_ref.shape[0] // BLOCK, block, 0)
     total = acc[...]
-    local = total[:, :slots] * 64.0 + total[:, slots : 2 * slots]
-    source = total[:, 2 * slots : 3 * slots] * 128.0 + total[:, 3 * slots :]
-    source_ref[...] = source.astype(I32)
-
+    first, second, third = (
+        total[:, slots * p : slots * (p + 1)].astype(I32) for p in range(3)
+    )
+    code = (first << 18) + ((second + 256) << 9) + third + 256
+    local, source = code & 2047, code >> 11
+    for p in range(2):
+        source_ref[pl.ds(p, devices, stride=2), :] = source[:, 128 * p : 128 * (p + 1)]
     index2 = set2_ref[...]
     home2 = home2_ref[...]
     marks2 = one_hot_rows(home2.shape[0], index2 >> 7)
@@ -121,7 +124,9 @@
     extra = lax.dot_general(
         member2.astype(F32).astype(BF16), value2, NT, preferred_element_type=F32
     )
-    want_ref[...] = (local + 2048.0 * extra).astype(I32)
+    wanted = local + (extra.astype(I32) << 11)
+    for p in range(2):
+        want_ref[:, p, :] = wanted[:, 128 * p : 128 * (p + 1)]
 
 
 def route(opp_set, opp_home, br_set, br_home, devices, slots):
@@ -129,14 +134,14 @@
     return pl.pallas_call(
         route_kernel,
         out_shape=(
-            jax.ShapeDtypeStruct((devices, slots), I32),
-            jax.ShapeDtypeStruct((devices, slots), I32),
+            jax.ShapeDtypeStruct((devices, 2, slots // 2), I32),
+            jax.ShapeDtypeStruct((2 * devices, slots // 2), I32),
             jax.ShapeDtypeStruct((hist // 128, 128), I32),
             jax.ShapeDtypeStruct((1, 128), I32),
         ),
         scratch_shapes=[
-            pltpu.VMEM((256, opp_home.shape[0] // 128), BF16),
-            pltpu.VMEM((devices, 4 * slots), F32),
+            pltpu.VMEM((1024, opp_home.shape[0] // 512), BF16),
+            pltpu.VMEM((devices, 3 * slots), F32),
             pltpu.VMEM((devices, 128), F32),
         ],
         name="route",
@@ -189,16 +194,27 @@
 
     my = number(me)
 
+    def rem(x, n):
+        return lax.rem(x, jnp.int32(n))
+
+    def div(x, n):
+        return lax.div(x, jnp.int32(n))
+
     def shift(i):
-        q, s = i // 2, 2 * (i % 2)
-        return q % 4 + s, (q // 32 + i) % 2, (q + q // 4) % 4 + s, (q + q // 16) % 2 + s
+        q, s = div(i, 2), 2 * rem(i, 2)
+        return (
+            rem(q, 4) + s,
+            rem(div(q, 32) + i, 2),
+            rem(q + div(q, 4), 4) + s,
+            rem(q + div(q, 16), 2) + s,
+        )
 
     def to(i):
-        c = tuple((m + d) % n for m, d, n in zip(me, shift(i), sizes))
+        c = tuple(rem(m + d, n) for m, d, n in zip(me, shift(i), sizes))
         return c, number(c)
 
     def back(i):
-        return number(tuple((m + 2 * n - d) % n for m, d, n in zip(me, shift(i), sizes)))
+        return number(tuple(rem(m + 2 * n - d, n) for m, d, n in zip(me, shift(i), sizes)))
 
     def copy(src, dst, out_sem, in_sem, device):
         return pltpu.make_async_remote_copy(
@@ -226,6 +242,14 @@
     each(request)
     asked[my] = want_ref[my]
     wide[...] = child_ref[...].astype(F32)
+    places = place_ref[...]
+    look_up(
+        jnp.concatenate(
+            [((places >> 8) * 256).astype(F32).astype(BF16), (places & 255).astype(F32).astype(BF16)],
+            axis=0,
+        ),
+        128, next_ref, jump, lambda x: x & 127, lambda x: x >> 7, lambda x: x.astype(I32),
+    )
     most = pl.ds(0, devices - 1)
     copy(want_ref.at[most], asked.at[most], ask_out, ask_in, tuple(me)).wait()
     for p in range(2):
@@ -258,23 +282,14 @@
     launch(jnp.int32(devices - 1))
     recv[my] = served(my)
 
-    places = place_ref[...]
-    look_up(
-        jnp.concatenate(
-            [((places >> 8) * 256).astype(F32).astype(BF16), (places & 255).astype(F32).astype(BF16)],
-            axis=0,
-        ),
-        128, next_ref, jump, lambda x: x & 127, lambda x: x >> 7, lambda x: x.astype(I32),
-    )
-
     def consume(n):
         def some(g, _):
-            for q in range(16):
-                k = g * 16 + q
-                gathered[pl.ds(k, 1), :] = wide[pl.ds(source_ref[n * slots + k], 1), :]
+            row, start = 2 * n + g, pl.multiple_of(g * 128, 128)
+            for q in range(128):
+                gathered[pl.ds(start + q, 1), :] = wide[pl.ds(source_ref[row, q], 1), :]
             return 0
 
-        lax.fori_loop(0, slots // 16, some, 0)
+        lax.fori_loop(0, 2, some, 0)
 
     def finish(n):
         product = recv[n].astype(F32) * gathered[...]
@@ -294,7 +309,11 @@
     each(take)
     pieces = jnp.concatenate(split(sums[...]), axis=0)
     look_up(pieces, 128, jump, part, lambda x: x >> 8, lambda x: x & 255)
-    weighted = part[...] * reach_ref[...]
+    reach = jnp.sum(
+        jnp.where(rows_iota(128, 128) == lanes_iota(128, 128), reach_ref[...], 0.0),
+        axis=1, keepdims=True,
+    )
+    weighted = part[...] * reach
     high, low = split(weighted)
     for s in range(2):
         marks = (rows_iota(devices, 128) * 2 + s == place2_ref[...]).astype(F32).astype(BF16)
@@ -324,7 +343,7 @@
     both = jnp.where(
         lane == 0,
         jnp.sum(gap_row, axis=1, keepdims=True),
-        jnp.where(lane == 1, jnp.sum(reach_ref[...], axis=0, keepdims=True), 0.0),
+        jnp.where(lane == 1, jnp.sum(reach_ref[...], axis=1, keepdims=True), 0.0),
     )
     parts[my] = both
     total_ref[...] = both
@@ -343,7 +362,7 @@
 
 
 def exchange(sizes, source, want, place, child_row, place2, reach, opp_cum, br_cum, child_value):
-    devices, slots = want.shape
+    devices, slots = want.shape[0], want.shape[1] * want.shape[2]
     hist, acts = child_value.shape
     rows = opp_cum.shape[0] // 4
     vmem, smem = pl.BlockSpec(memory_space=pltpu.VMEM), pl.BlockSpec(memory_space=pltpu.SMEM)
@@ -376,12 +395,12 @@
         compiler_params=pltpu.CompilerParams(collective_id=0, has_side_effects=True),
         name="exchange",
     )(
-        source.reshape(-1),
-        want.reshape(devices, 2, 128),
+        source,
+        want,
         place,
         child_row.reshape(-1, 128),
         place2,
-        reach.reshape(-1, 1),
+        reach.reshape(1, -1),
         opp_cum,
         br_cum,
         child_value,

time: 238 us -> 215 us (0.903)
  Pallas kernels: 228 us -> 208 us
  local copies, waits for them, and re-layouts: 7.27 us -> 2.59 us
    pallas_call x1, Pallas kernels: 189 us -> 169 us  [exchange(): pl.pallas_call(functools.partial(exchange_kernel, sizes), in_specs=[smem]...]
    reshape x2 -> x0, local copies, waits for them, and re-layouts: 3 us -> none  [the longest x1 1.61 us: exchange(): want.reshape(devices, 2, 128)]
where the time goes in v3:
time: 215 us; the launch traced here: 213 us
  Pallas kernels  208 us (97%)
  local copies, waits for them, and re-layouts  2.59 us (1%)
  between operations  2.4 us (1%)
    pallas_call x1, Pallas kernels, exchange(): pl.pallas_call(functools.partial(exchange_kernel, sizes), in_specs=[smem]...  169 us
    pallas_call x1, Pallas kernels, route(): pl.pallas_call(route_kernel, out_shape=(jax.ShapeDtypeStruct((devices, 2,...  39.3 us

profile of v3, /device:TPU:0, one launch (start us, length us, event | category | flops | bytes accessed | tf_op | source)
XLA Modules:
  0.0 213.4 jit_solution(777615691425475919)
XLA Ops:
  0.6 39.3 %route.1 = (s32[128,2,128]{2,1,0:T(2,128)}, s32[256,128]{1,0:T(8,128)}, s32[128,128]{1,0:T(8,128)}, s32[1,128]{1,0:T(1,128)}) custom-call(s32[128,128]{1,0:T(8,128)} %bitcast.12, s32[2048,128]{1,0:T(8,128)} %bitcast.10, s32[1,128]{1,0:T(1,128)} %bitcast.15, s32[64,128]{1,0:T(8,128)} %bitcast.14), custom_call_target="tpu_custom_call" | custom-call | tf_op jit(solution)/shard_map/route/pallas_call | solution.py:134
  40.0 169.1 %exchange.1 = (f32[128,128]{1,0:T(8,128)}, f32[1,64]{1,0:T(1,128)}, f32[1,128]{1,0:T(1,128)}) custom-call(s32[256,128]{1,0:T(8,128)} %get-tuple-element.10.source_ref, s32[128,2,128]{2,1,0:T(2,128)} %get-tuple-element.11.want_ref, s32[128,128]{1,0:T(8,128)} %get-tuple-element.12.place_ref, s32[128,128]{1,0:T(8,128)} %bitcast.11, ...), custom_call_target="tpu_custom_call" | custom-call | tf_op jit(solution)/shard_map/exchange/pallas_call | solution.py:370
  209.1 1.5 copy.15
  210.6 1.1 copy.16

commit v4 on v3

--- a/solution.py
+++ b/solution.py
@@ -59,13 +59,19 @@
         at = pl.ds(pl.multiple_of(b * BLOCK, BLOCK), BLOCK)
         index = set_ref[at, :]
         high, low = index >> 9, index & 511
-        marks = jnp.concatenate(
-            [one_hot_rows(wide, high[j : j + 1, :]) for j in range(BLOCK)], axis=1
-        )
-        found = dot(table[...], marks)
+        each = BLOCK // 2
+        marks = [
+            jnp.concatenate(
+                [one_hot_rows(wide, high[j : j + 1, :]) for j in range(h * each, (h + 1) * each)],
+                axis=1,
+            )
+            for h in range(2)
+        ]
+        halves = [dot(table[...], m) for m in marks]
         members, values = [], []
         for j in range(BLOCK):
-            lanes = slice(128 * j, 128 * (j + 1))
+            found, at_lane = halves[j // each], j % each
+            lanes = slice(128 * at_lane, 128 * (at_lane + 1))
             mine = low[j : j + 1, :]
             top = pick(found[0:512, lanes], mine).astype(I32) + 256
             bottom = pick(found[512:1024, lanes], mine).astype(I32) + 256
@@ -184,8 +190,8 @@
                     cum_ref, br_ref, child_ref,
                     value_ref, gap_ref, total_ref,
                     asked, columns, table, wide, send, recv, gathered, sums, jump,
-                    outgoing, incoming, part, parts,
-                    ask_out, ask_in, row_out, row_in, act_out, act_in, sum_out, sum_in):
+                    outgoing, incoming, part, parts_one, parts_two, middle_ref, ask_mid, act_mid,
+                    ask_sems, row_out, row_in, act_sems, sum_sems):
     devices, slots, acts = send.shape
     me = [lax.axis_index(a) for a in AXES]
 
@@ -235,13 +241,47 @@
         table[:, 128 * p : 128 * (p + 1)] = policy.astype(BF16)
     pl.semaphore_wait(barrier, devices - 1)
 
-    def request(i):
-        device, n = to(i)
-        copy(want_ref.at[n], asked.at[my], ask_out, ask_in, device).start()
-
-    each(request)
-    asked[my] = want_ref[my]
+    first, second = me[0] * sizes[1] + me[1], me[2] * sizes[3] + me[3]
+    near, far = sizes[0] * sizes[1], sizes[2] * sizes[3]
+
+    def along_first(t):
+        c = rem(me[0] + div(t, sizes[1]), sizes[0]), rem(me[1] + rem(t, sizes[1]), sizes[1])
+        return (*c, me[2], me[3]), c[0] * sizes[1] + c[1]
+
+    def along_second(t):
+        c = rem(me[2] + div(t, sizes[3]), sizes[2]), rem(me[3] + rem(t, sizes[3]), sizes[3])
+        return (me[0], me[1], *c), c[0] * sizes[3] + c[1]
+
+    def over(count, body):
+        lax.fori_loop(1, count, lambda t, c: (body(t), c)[1], 0)
+
+    def stage_one(source, middle, sems):
+        def go(t):
+            device, n = along_first(t)
+            copy(source.at[n], middle.at[first], sems.at[0], sems.at[1], device).start()
+
+        over(near, go)
+        middle[first] = source[first]
+
+    def stage_two(middle, target, sems):
+        some = pl.ds(0, near - 1)
+        copy(middle.at[some], middle.at[some], sems.at[0], sems.at[1], tuple(me)).wait()
+
+        def go(t):
+            device, n = along_second(t)
+            copy(middle.at[:, n], target.at[:, second], sems.at[2], sems.at[3], device).start()
+
+        over(far, go)
+        target[:, second] = middle[:, second]
+
+    def stage_end(middle, target, sems):
+        some = pl.ds(0, far - 1)
+        copy(middle.at[:, some], target.at[:, some], sems.at[2], sems.at[3], tuple(me)).wait()
+
+    most = pl.ds(0, devices - 1)
+    stage_one(want_ref, ask_mid, ask_sems)
     wide[...] = child_ref[...].astype(F32)
+    stage_two(ask_mid, asked, ask_sems)
     places = place_ref[...]
     look_up(
         jnp.concatenate(
@@ -251,9 +291,10 @@
         128, next_ref, jump, lambda x: x & 127, lambda x: x >> 7, lambda x: x.astype(I32),
     )
     most = pl.ds(0, devices - 1)
-    copy(want_ref.at[most], asked.at[most], ask_out, ask_in, tuple(me)).wait()
+    stage_end(ask_mid, asked, ask_sems)
     for p in range(2):
-        columns[128 * p : 128 * (p + 1), :] = asked[:, p, :].astype(F32).T.astype(I32)
+        rowwise = asked[:, :, p, :].reshape(devices, 128)
+        columns[128 * p : 128 * (p + 1), :] = rowwise.astype(F32).T.astype(I32)
 
     def served(n):
         column = jnp.sum(
@@ -317,21 +358,17 @@
     high, low = split(weighted)
     for s in range(2):
         marks = (rows_iota(devices, 128) * 2 + s == place2_ref[...]).astype(F32).astype(BF16)
-        outgoing[:, s, :] = dot(marks, high) + dot(marks, low)
-
-    def act(i):
-        device, n = to(i)
-        copy(outgoing.at[n], incoming.at[my], act_out, act_in, device).start()
-
-    each(act)
-    incoming[my] = outgoing[my]
+        outgoing[:, :, s, :] = (dot(marks, high) + dot(marks, low)).reshape(near, far, acts)
+
+    stage_one(outgoing, act_mid, act_sems)
+    stage_two(act_mid, incoming, act_sems)
     look_up(pieces, 128, place_ref, value_ref, lambda x: x >> 8, lambda x: x & 255)
-    copy(outgoing.at[most], incoming.at[most], act_out, act_in, tuple(me)).wait()
+    stage_end(act_mid, incoming, act_sems)
     action = jnp.zeros((br_ref.shape[0], acts), F32)
     for s in range(2):
         owned = columns[s : s + 1, :] >> 11
         member = (rows_iota(br_ref.shape[0], devices) + 1 == owned).astype(F32).astype(BF16)
-        high, low = split(incoming[:, s, :])
+        high, low = split(incoming[:, :, s, :].reshape(devices, acts))
         action += dot(member, high) + dot(member, low)
     br = br_ref[...]
     br_policy = br / jnp.sum(br, axis=1, keepdims=True)
@@ -345,16 +382,26 @@
         jnp.sum(gap_row, axis=1, keepdims=True),
         jnp.where(lane == 1, jnp.sum(reach_ref[...], axis=1, keepdims=True), 0.0),
     )
-    parts[my] = both
+    parts_one[first] = both
     total_ref[...] = both
 
-    def tell(i):
-        device, n = to(i)
-        copy(total_ref, parts.at[my], sum_out, sum_in, device).start()
-
-    each(tell)
-    copy(parts.at[most], parts.at[most], sum_out, sum_in, tuple(me)).wait()
-    total = jnp.sum(parts[:, 0, :], axis=0, keepdims=True)
+    def tell_first(t):
+        copy(total_ref, parts_one.at[first], sum_sems.at[0], sum_sems.at[1], along_first(t)[0]).start()
+
+    over(near, tell_first)
+    some = pl.ds(0, near - 1)
+    copy(parts_one.at[some], parts_one.at[some], sum_sems.at[0], sum_sems.at[1], tuple(me)).wait()
+    middle = jnp.sum(parts_one[:, 0, :], axis=0, keepdims=True)
+    parts_two[second] = middle
+    middle_ref[...] = middle
+
+    def tell_second(t):
+        copy(middle_ref, parts_two.at[second], sum_sems.at[2], sum_sems.at[3], along_second(t)[0]).start()
+
+    over(far, tell_second)
+    some = pl.ds(0, far - 1)
+    copy(parts_two.at[some], parts_two.at[some], sum_sems.at[2], sum_sems.at[3], tuple(me)).wait()
+    total = jnp.sum(parts_two[:, 0, :], axis=0, keepdims=True)
     top = jnp.sum(jnp.where(lane == 0, total, 0.0), axis=1, keepdims=True)
     bottom = jnp.sum(jnp.where(lane == 1, total, 0.0), axis=1, keepdims=True)
     total_ref[...] = jnp.broadcast_to(top / bottom, (1, 128))
@@ -365,6 +412,7 @@
     devices, slots = want.shape[0], want.shape[1] * want.shape[2]
     hist, acts = child_value.shape
     rows = opp_cum.shape[0] // 4
+    near, far = sizes[0] * sizes[1], sizes[2] * sizes[3]
     vmem, smem = pl.BlockSpec(memory_space=pltpu.VMEM), pl.BlockSpec(memory_space=pltpu.SMEM)
     dma = pltpu.SemaphoreType.DMA
     return pl.pallas_call(
@@ -377,7 +425,7 @@
             jax.ShapeDtypeStruct((1, 128), F32),
         ),
         scratch_shapes=[
-            pltpu.VMEM((devices, 2, 128), I32),
+            pltpu.VMEM((near, far, 2, 128), I32),
             pltpu.VMEM((slots, devices), I32),
             pltpu.VMEM((rows, 4 * acts), BF16),
             pltpu.VMEM((hist, acts), F32),
@@ -386,17 +434,21 @@
             pltpu.VMEM((slots, acts), F32),
             pltpu.VMEM((slots, devices), F32),
             pltpu.VMEM((128, 128), I32),
-            pltpu.VMEM((devices, 2, acts), F32),
-            pltpu.VMEM((devices, 2, acts), F32),
+            pltpu.VMEM((near, far, 2, acts), F32),
+            pltpu.VMEM((near, far, 2, acts), F32),
             pltpu.VMEM((128, 128), F32),
-            pltpu.VMEM((devices, 1, 128), F32),
-            dma, dma, dma, dma((devices,)), dma, dma, dma, dma,
+            pltpu.VMEM((near, 1, 128), F32),
+            pltpu.VMEM((far, 1, 128), F32),
+            pltpu.VMEM((1, 128), F32),
+            pltpu.VMEM((near, far, 2, 128), I32),
+            pltpu.VMEM((near, far, 2, acts), F32),
+            dma((4,)), dma, dma((devices,)), dma((4,)), dma((4,)),
         ],
         compiler_params=pltpu.CompilerParams(collective_id=0, has_side_effects=True),
         name="exchange",
     )(
         source,
-        want,
+        want.reshape(near, far, 2, 128),
         place,
         child_row.reshape(-1, 128),
         place2,

time: 215 us -> 206 us (0.958)
  Pallas kernels: 208 us -> 201 us
    pallas_call x1, Pallas kernels: 169 us -> 162 us  [exchange(): pl.pallas_call(functools.partial(exchange_kernel, sizes), in_specs=[smem]...]
where the time goes in v4:
time: 206 us
  Pallas kernels  201 us (98%)
  local copies, waits for them, and re-layouts  2.59 us (1%)
  between operations  2.4 us (1%)
    pallas_call x1, Pallas kernels, exchange(): pl.pallas_call(functools.partial(exchange_kernel, sizes), in_specs=[smem]...  162 us
    pallas_call x1, Pallas kernels, route(): pl.pallas_call(route_kernel, out_shape=(jax.ShapeDtypeStruct((devices, 2,...  39.3 us

profile of v4, /device:TPU:0, one launch (start us, length us, event | category | flops | bytes accessed | tf_op | source)
XLA Modules:
  0.0 206.1 jit_solution(6832160691821121522)
XLA Ops:
  0.6 39.3 %route.1 = (s32[128,2,128]{2,1,0:T(2,128)}, s32[256,128]{1,0:T(8,128)}, s32[128,128]{1,0:T(8,128)}, s32[1,128]{1,0:T(1,128)}) custom-call(s32[128,128]{1,0:T(8,128)} %bitcast.14, s32[2048,128]{1,0:T(8,128)} %bitcast.11, s32[1,128]{1,0:T(1,128)} %bitcast.17, s32[64,128]{1,0:T(8,128)} %bitcast.16), custom_call_target="tpu_custom_call" | custom-call | tf_op jit(solution)/shard_map/route/pallas_call | solution.py:140
  40.0 161.8 %exchange.1 = (f32[128,128]{1,0:T(8,128)}, f32[1,64]{1,0:T(1,128)}, f32[1,128]{1,0:T(1,128)}) custom-call(s32[256,128]{1,0:T(8,128)} %get-tuple-element.10.source_ref, s32[8,16,2,128]{3,2,1,0:T(2,128)} %bitcast.12, s32[128,128]{1,0:T(8,128)} %get-tuple-element.12.place_ref, s32[128,128]{1,0:T(8,128)} %bitcast.13, s32[1,128]{1,0:T(1,128)} %get-tuple-element.13.place2_ref, ...), custom_call_target="tpu_custom_call" | custom-call | tf_op jit(solution)/shard_map/exchange/pallas_call | solution.py:418
  201.8 1.5 copy.15
  203.2 1.1 copy.16

commit v5 on v4

--- a/solution.py
+++ b/solution.py
@@ -42,13 +42,12 @@
                  want_ref, source_ref, place_ref, place2_ref,
                  table, acc, carry):
     devices, slots = want_ref.shape[0], 256
-    wide = table.shape[1]
+    wide = table.shape[1] // 2
     for q in range(4):
         home = home_ref[pl.ds(q, wide, stride=4), :]
-        table[128 * q : 128 * (q + 1), :] = ((home >> 9) - 256).astype(F32).T.astype(BF16)
-        table[512 + 128 * q : 512 + 128 * (q + 1), :] = (
-            ((home & 511) - 256).astype(F32).T.astype(BF16)
-        )
+        lanes = slice(128 * q, 128 * (q + 1))
+        table[lanes, :wide] = (((home >> 9) - 256) * 512).astype(F32).T.astype(BF16)
+        table[lanes, wide:] = ((home & 511) - 256).astype(F32).T.astype(BF16)
     acc[...] = jnp.zeros_like(acc)
     carry[...] = jnp.zeros_like(carry)
     upper = jnp.concatenate(
@@ -67,15 +66,13 @@
             )
             for h in range(2)
         ]
-        halves = [dot(table[...], m) for m in marks]
+        halves = [dot(table[...], jnp.concatenate([m, m], axis=0)) for m in marks]
         members, values = [], []
         for j in range(BLOCK):
             found, at_lane = halves[j // each], j % each
             lanes = slice(128 * at_lane, 128 * (at_lane + 1))
             mine = low[j : j + 1, :]
-            top = pick(found[0:512, lanes], mine).astype(I32) + 256
-            bottom = pick(found[512:1024, lanes], mine).astype(I32) + 256
-            row = (top << 9) + bottom
+            row = pick(found[:, lanes], mine).astype(I32) + (256 * 512 + 256)
             owner, local = row >> 11, row & 2047
             member = rows_iota(128, 128) == owner
             member16 = member.astype(F32).astype(BF16)
@@ -146,7 +143,7 @@
             jax.ShapeDtypeStruct((1, 128), I32),
         ),
         scratch_shapes=[
-            pltpu.VMEM((1024, opp_home.shape[0] // 512), BF16),
+            pltpu.VMEM((512, opp_home.shape[0] // 256), BF16),
             pltpu.VMEM((devices, 3 * slots), F32),
             pltpu.VMEM((devices, 128), F32),
         ],
@@ -168,22 +165,21 @@
     marks = jnp.concatenate(
         [one_hot_rows(rows, high_of(index[j : j + 1, :])) for j in range(BLOCK)], axis=1
     )
-    found = dot(pieces, marks)
-    half = found.shape[0] // 2
-    both = found[:half, :] + found[half:, :]
+    both = dot(pieces, jnp.concatenate([marks, marks], axis=0))
     return [
         pick(both[:, 128 * j : 128 * (j + 1)], low_of(index[j : j + 1, :])) for j in range(BLOCK)
     ]
 
 
-def look_up(pieces, rows, index_ref, out_ref, high_of, low_of, cast=lambda x: x):
+def look_up(pieces, rows, index_ref, out_ref, high_of, low_of, cast=lambda x: x, part=(0, 2)):
     def block(b, _):
         at = pl.ds(pl.multiple_of(b * BLOCK, BLOCK), BLOCK)
         for j, row in enumerate(find(pieces, rows, index_ref[at, :], high_of, low_of)):
             out_ref[pl.ds(b * BLOCK + j, 1), :] = cast(row)
         return 0
 
-    lax.fori_loop(0, index_ref.shape[0] // BLOCK, block, 0)
+    half = index_ref.shape[0] // BLOCK // 2
+    lax.fori_loop(part[0] * half, part[1] * half, block, 0)
 
 
 def exchange_kernel(sizes, source_ref, want_ref, place_ref, next_ref, place2_ref, reach_ref,
@@ -191,7 +187,7 @@
                     value_ref, gap_ref, total_ref,
                     asked, columns, table, wide, send, recv, gathered, sums, jump,
                     outgoing, incoming, part, parts_one, parts_two, middle_ref, ask_mid, act_mid,
-                    ask_sems, row_out, row_in, act_sems, sum_sems):
+                    child16, child_sem, ask_sems, row_out, row_in, act_sems, sum_sems):
     devices, slots, acts = send.shape
     me = [lax.axis_index(a) for a in AXES]
 
@@ -231,6 +227,8 @@
     def each(body, first=1):
         lax.fori_loop(first, devices, lambda i, c: (body(i), c)[1], 0)
 
+    child_in = pltpu.make_async_copy(child_ref, child16, child_sem)
+    child_in.start()
     barrier = pltpu.get_barrier_semaphore()
     each(lambda i: pl.semaphore_signal(
         barrier, inc=1, device_id=to(i)[0], device_id_type=pl.DeviceIdType.MESH))
@@ -239,6 +237,17 @@
         cum = cum_ref[p * rows : (p + 1) * rows, :]
         policy = cum / jnp.sum(cum, axis=1, keepdims=True)
         table[:, 128 * p : 128 * (p + 1)] = policy.astype(BF16)
+    places = place_ref[...]
+    look_up(
+        jnp.concatenate(
+            [((places >> 8) * 256).astype(F32).astype(BF16), (places & 255).astype(F32).astype(BF16)],
+            axis=1,
+        ),
+        128, next_ref, jump, lambda x: x & 127, lambda x: x >> 7, lambda x: x.astype(I32),
+    )
+    most = pl.ds(0, devices - 1)
+    child_in.wait()
+    wide[...] = child16[...].astype(F32)
     pl.semaphore_wait(barrier, devices - 1)
 
     first, second = me[0] * sizes[1] + me[1], me[2] * sizes[3] + me[3]
@@ -280,17 +289,7 @@
 
     most = pl.ds(0, devices - 1)
     stage_one(want_ref, ask_mid, ask_sems)
-    wide[...] = child_ref[...].astype(F32)
     stage_two(ask_mid, asked, ask_sems)
-    places = place_ref[...]
-    look_up(
-        jnp.concatenate(
-            [((places >> 8) * 256).astype(F32).astype(BF16), (places & 255).astype(F32).astype(BF16)],
-            axis=0,
-        ),
-        128, next_ref, jump, lambda x: x & 127, lambda x: x >> 7, lambda x: x.astype(I32),
-    )
-    most = pl.ds(0, devices - 1)
     stage_end(ask_mid, asked, ask_sems)
     for p in range(2):
         rowwise = asked[:, :, p, :].reshape(devices, 128)
@@ -348,7 +347,7 @@
         finish(n)
 
     each(take)
-    pieces = jnp.concatenate(split(sums[...]), axis=0)
+    pieces = jnp.concatenate(split(sums[...]), axis=1)
     look_up(pieces, 128, jump, part, lambda x: x >> 8, lambda x: x & 255)
     reach = jnp.sum(
         jnp.where(rows_iota(128, 128) == lanes_iota(128, 128), reach_ref[...], 0.0),
@@ -361,8 +360,9 @@
         outgoing[:, :, s, :] = (dot(marks, high) + dot(marks, low)).reshape(near, far, acts)
 
     stage_one(outgoing, act_mid, act_sems)
+    look_up(pieces, 128, place_ref, value_ref, lambda x: x >> 8, lambda x: x & 255, part=(0, 1))
     stage_two(act_mid, incoming, act_sems)
-    look_up(pieces, 128, place_ref, value_ref, lambda x: x >> 8, lambda x: x & 255)
+    look_up(pieces, 128, place_ref, value_ref, lambda x: x >> 8, lambda x: x & 255, part=(1, 2))
     stage_end(act_mid, incoming, act_sems)
     action = jnp.zeros((br_ref.shape[0], acts), F32)
     for s in range(2):
@@ -417,7 +417,7 @@
     dma = pltpu.SemaphoreType.DMA
     return pl.pallas_call(
         functools.partial(exchange_kernel, sizes),
-        in_specs=[smem] + [vmem] * 8,
+        in_specs=[smem] + [vmem] * 7 + [pl.BlockSpec(memory_space=pl.ANY)],
         out_specs=[vmem] * 3,
         out_shape=(
             jax.ShapeDtypeStruct((hist // 128, 128), F32),
@@ -442,7 +442,8 @@
             pltpu.VMEM((1, 128), F32),
             pltpu.VMEM((near, far, 2, 128), I32),
             pltpu.VMEM((near, far, 2, acts), F32),
-            dma((4,)), dma, dma((devices,)), dma((4,)), dma((4,)),
+            pltpu.VMEM((hist, acts), BF16),
+            dma, dma((4,)), dma, dma((devices,)), dma((4,)), dma((4,)),
         ],
         compiler_params=pltpu.CompilerParams(collective_id=0, has_side_effects=True),
         name="exchange",

time: 206 us -> 202 us (0.981)
  Pallas kernels: 201 us -> 196 us
    pallas_call x1, Pallas kernels: 162 us -> 156 us  [exchange(): pl.pallas_call(functools.partial(exchange_kernel, sizes), in_specs=[smem]...]
where the time goes in v5:
time: 202 us; the launch traced here: 201 us
  Pallas kernels  196 us (97%)
  local copies, waits for them, and re-layouts  2.59 us (1%)
  between operations  2.4 us (1%)
    pallas_call x1, Pallas kernels, exchange(): pl.pallas_call(functools.partial(exchange_kernel, sizes), in_specs=[smem]...  156 us
    pallas_call x1, Pallas kernels, route(): pl.pallas_call(route_kernel, out_shape=(jax.ShapeDtypeStruct((devices, 2,...  40.2 us

profile of v5, /device:TPU:0, one launch (start us, length us, event | category | flops | bytes accessed | tf_op | source)
XLA Modules:
  0.0 201.4 jit_solution(9076942640309473681)
XLA Ops:
  0.6 40.2 %route.1 = (s32[128,2,128]{2,1,0:T(2,128)}, s32[256,128]{1,0:T(8,128)}, s32[128,128]{1,0:T(8,128)}, s32[1,128]{1,0:T(1,128)}) custom-call(s32[128,128]{1,0:T(8,128)} %bitcast.14, s32[2048,128]{1,0:T(8,128)} %bitcast.11, s32[1,128]{1,0:T(1,128)} %bitcast.17, s32[64,128]{1,0:T(8,128)} %bitcast.16), custom_call_target="tpu_custom_call" | custom-call | tf_op jit(solution)/shard_map/route/pallas_call | solution.py:137
  40.8 156.2 %exchange.1 = (f32[128,128]{1,0:T(8,128)}, f32[1,64]{1,0:T(1,128)}, f32[1,128]{1,0:T(1,128)}) custom-call(s32[256,128]{1,0:T(8,128)} %get-tuple-element.10.source_ref, s32[8,16,2,128]{3,2,1,0:T(2,128)} %bitcast.12, s32[128,128]{1,0:T(8,128)} %get-tuple-element.12.place_ref, s32[128,128]{1,0:T(8,128)} %bitcast.13, s32[1,128]{1,0:T(1,128)} %get-tuple-element.13.place2_ref, ...), custom_call_target="tpu_custom_call" | custom-call | tf_op jit(solution)/shard_map/exchange/pallas_call | solution.py:418
  197.1 1.5 copy.15
  198.5 1.1 copy.16

commit v6 on v5

--- a/solution.py
+++ b/solution.py
@@ -95,8 +95,8 @@
             )
             members.append(member16)
         acc[...] += lax.dot_general(
+            jnp.concatenate(values, axis=1),
             jnp.concatenate(members, axis=1),
-            jnp.concatenate(values, axis=1),
             NT,
             preferred_element_type=F32,
         )
@@ -105,7 +105,7 @@
     lax.fori_loop(0, set_ref.shape[0] // BLOCK, block, 0)
     total = acc[...]
     first, second, third = (
-        total[:, slots * p : slots * (p + 1)].astype(I32) for p in range(3)
+        total[slots * p : slots * (p + 1), :].T.astype(I32) for p in range(3)
     )
     code = (first << 18) + ((second + 256) << 9) + third + 256
     local, source = code & 2047, code >> 11
@@ -144,7 +144,7 @@
         ),
         scratch_shapes=[
             pltpu.VMEM((512, opp_home.shape[0] // 256), BF16),
-            pltpu.VMEM((devices, 3 * slots), F32),
+            pltpu.VMEM((3 * slots, devices), F32),
             pltpu.VMEM((devices, 128), F32),
         ],
         name="route",

time: 202 us -> 196 us (0.970)
  Pallas kernels: 196 us -> 191 us
    pallas_call x1, Pallas kernels: 40.2 us -> 36.6 us  [route(): pl.pallas_call(route_kernel, out_shape=(jax.ShapeDtypeStruct((devices, 2,...]
    pallas_call x1, Pallas kernels: 156 us -> 154 us  [exchange(): pl.pallas_call(functools.partial(exchange_kernel, sizes), in_specs=[smem]...]
where the time goes in v6:
time: 196 us
  Pallas kernels  191 us (97%)
  local copies, waits for them, and re-layouts  2.59 us (1%)
  between operations  2.4 us (1%)
    pallas_call x1, Pallas kernels, exchange(): pl.pallas_call(functools.partial(exchange_kernel, sizes), in_specs=[smem]...  154 us
    pallas_call x1, Pallas kernels, route(): pl.pallas_call(route_kernel, out_shape=(jax.ShapeDtypeStruct((devices, 2,...  36.6 us

profile of v6, /device:TPU:0, one launch (start us, length us, event | category | flops | bytes accessed | tf_op | source)
XLA Modules:
  0.0 195.8 jit_solution(6169224345649875443)
XLA Ops:
  0.6 36.6 %route.1 = (s32[128,2,128]{2,1,0:T(2,128)}, s32[256,128]{1,0:T(8,128)}, s32[128,128]{1,0:T(8,128)}, s32[1,128]{1,0:T(1,128)}) custom-call(s32[128,128]{1,0:T(8,128)} %bitcast.14, s32[2048,128]{1,0:T(8,128)} %bitcast.11, s32[1,128]{1,0:T(1,128)} %bitcast.17, s32[64,128]{1,0:T(8,128)} %bitcast.16), custom_call_target="tpu_custom_call" | custom-call | tf_op jit(solution)/shard_map/route/pallas_call | solution.py:137
  37.3 154.2 %exchange.1 = (f32[128,128]{1,0:T(8,128)}, f32[1,64]{1,0:T(1,128)}, f32[1,128]{1,0:T(1,128)}) custom-call(s32[256,128]{1,0:T(8,128)} %get-tuple-element.10.source_ref, s32[8,16,2,128]{3,2,1,0:T(2,128)} %bitcast.12, s32[128,128]{1,0:T(8,128)} %get-tuple-element.12.place_ref, s32[128,128]{1,0:T(8,128)} %bitcast.13, s32[1,128]{1,0:T(1,128)} %get-tuple-element.13.place2_ref, ...), custom_call_target="tpu_custom_call" | custom-call | tf_op jit(solution)/shard_map/exchange/pallas_call | solution.py:418
  191.4 1.5 copy.15
  192.9 1.1 copy.16
